TPU v7x, 32 devices: a whole 2x2x4 slice. The times are simulated.
32 devices in a mesh: text: 2 (over core), tag: 16 (over z, y, x).
Axes of the slice: x: 2, y: 2, z: 4, core: 2. Of those that a mesh axis runs over, the one named last changes fastest.
Arguments:
- tile_values: bfloat16 [2, 160, 512, 512], P('text', 'tag'), may hold values from -0.1875 to 0.1875
- tile_rows: int32 [2, 160], P('text', 'tag'), may hold values from 0 to 3, as said below
- tile_cols: int32 [2, 160], P('text', 'tag'), may hold values from 0 to 2, as said below
- tile_counts: int32 [2, 16], P('text', 'tag'), may hold values from 1 to 10, as said below
- panel_init: bfloat16 [4096, 512], P(('text', 'tag')), may hold values from -6 to 6
Outputs:
- text_white: float32 [4096, 512], P(('text', 'tag'))
- tag_white: float32 [24576, 512], P(('tag', 'text'))
Inputs may be any that keep to these rules, and one draw needn't show every extreme that they name: `tile_rows`: within one pair of blocks the live slots name distinct tile positions. `tile_cols`: within one pair of blocks the live slots name distinct tile positions. `tile_counts`: in every draw some pair of blocks holds exactly 10 tiles.
All inputs are finite; a program needn't handle non-finite values.
Results may differ from a plain program's by a relative error of at most 0.005.
Values may be sent and summed in bfloat16 or wider, within the bound.
A program may use at most 64 MiB of HBM per device.

v0:
```python
import functools
import math

import jax
import jax.numpy as jnp
from jax import lax
from jax.experimental import pallas as pl
from jax.experimental.pallas import tpu as pltpu
from jax.sharding import PartitionSpec as P

TC = 3
LANES = 128
VMEM = pltpu.VMEM


def tag_kernel(rows, cols, count, tile, panel, out):
    slot = pl.program_id(0)
    width = tile.shape[1]

    @pl.when(slot == 0)
    def _():
        out[...] = jnp.zeros_like(out)

    @pl.when(slot < count[0])
    def _():
        source = panel[pl.ds(pl.multiple_of(rows[slot] * width, width), width), :]
        into = pl.ds(pl.multiple_of(cols[slot] * width, width), width)
        out[into, :] += lax.dot_general(
            tile[0], source, (((0,), (0,)), ((), ())), preferred_element_type=jnp.float32
        )


def text_kernel(rows, cols, count, tile, panel, out, total):
    slot = pl.program_id(0)
    width = tile.shape[1]

    @pl.when(slot == 0)
    def _():
        total[...] = jnp.zeros_like(total)

    @pl.when(slot < count[0])
    def _():
        source = panel[pl.ds(pl.multiple_of(cols[slot] * width, width), width), :]
        into = pl.ds(pl.multiple_of(rows[slot] * width, width), width)
        total[into, :] += jnp.dot(tile[0], source, preferred_element_type=jnp.float32)

    @pl.when(slot == pl.num_programs(0) - 1)
    def _():
        out[...] = total[...].astype(out.dtype)


def tile_product(kernel, tiles, rows, cols, count, panel, out_rows, out_type, scratch):
    slots, width, _ = tiles.shape
    comps = panel.shape[1]

    def tile_at(slot, rows, cols, count):
        return (jnp.minimum(slot, count[0] - 1), 0, 0)

    def whole(slot, rows, cols, count):
        return (0, 0)

    return pl.pallas_call(
        kernel,
        out_shape=jax.ShapeDtypeStruct((out_rows, comps), out_type),
        grid_spec=pltpu.PrefetchScalarGridSpec(
            num_scalar_prefetch=3,
            grid=(slots,),
            in_specs=[
                pl.BlockSpec((1, width, width), tile_at),
                pl.BlockSpec(panel.shape, whole),
            ],
            out_specs=pl.BlockSpec((out_rows, comps), whole),
            scratch_shapes=scratch,
        ),
        compiler_params=pltpu.CompilerParams(vmem_limit_bytes=20 << 20),
    )(rows, cols, count, tiles, panel)


def eliminate(block):
    size = block.shape[0]
    groups = size // 8
    lane = lax.broadcasted_iota(jnp.int32, (8, size), 1)
    sub = lax.broadcasted_iota(jnp.int32, (8, size), 0)
    m = [block[8 * g : 8 * g + 8, :] for g in range(groups)]
    pivots = []

    def across(rows, k):
        return jnp.broadcast_to(rows[:, k : k + 1], (8, size))

    def down(rows, s):
        return jnp.broadcast_to(rows[s : s + 1, :], (8, size))

    for g in range(groups):
        at = 8 * g
        inside = (lane >= at) & (lane < at + 8)
        own = [across(m[g], at + t) for t in range(8)]
        entry = {(s, t): down(own[t], s) for t in range(8) for s in range(t, 8)}
        start = jnp.where(inside, jnp.where(lane == sub + at, 1.0, 0.0), m[g])
        rows = [down(start, s) for s in range(8)]
        ratio, inverse, scaled = {}, [], []
        for t in range(8):
            inverse.append(1.0 / entry[t, t])
            for s in range(t + 1, 8):
                ratio[s, t] = entry[s, t] * inverse[t]
            for q in range(t + 1, 8):
                for s in range(q, 8):
                    entry[s, q] = entry[s, q] - ratio[q, t] * entry[s, t]
                rows[q] = rows[q] - ratio[q, t] * rows[t]
            scaled.append(rows[t] * inverse[t])
        for i in range(g + 1, groups):
            columns = [across(m[i], at + t) for t in range(8)]
            total = jnp.where(inside, 0.0, m[i])
            for t in range(8):
                for q in range(t + 1, 8):
                    columns[q] = columns[q] - ratio[q, t] * columns[t]
                total = total - columns[t] * scaled[t]
            m[i] = total
        done, pivot = rows[0], entry[0, 0]
        for t in range(1, 8):
            done = jnp.where(sub == t, rows[t], done)
            pivot = jnp.where(sub == t, entry[t, t], pivot)
        m[g] = done
        pivots.append(pivot)
    out = []
    for g in range(groups):
        kept = jnp.where(lane <= sub + 8 * g, m[g], 0.0)
        out.append(kept * lax.rsqrt(pivots[g]))
    return jnp.concatenate(out, axis=0)


def factor_kernel(gram, out, work):
    size = gram.shape[0]
    blocks = size // LANES
    work[...] = gram[...]
    exact = lax.Precision.HIGHEST

    for b in range(blocks):
        lo, hi = b * LANES, (b + 1) * LANES
        inverse = eliminate(work[lo:hi, lo:hi])
        row = jnp.dot(
            inverse, work[lo:hi, :], preferred_element_type=jnp.float32, precision=exact
        )
        work[lo:hi, :] = row
        work[lo:hi, lo:hi] = inverse
        if hi < size:
            work[hi:, lo:hi] = jnp.zeros((size - hi, LANES), jnp.float32)
            work[hi:, :] -= lax.dot_general(
                work[lo:hi, hi:],
                work[lo:hi, :],
                (((0,), (0,)), ((), ())),
                preferred_element_type=jnp.float32,
                precision=exact,
            )
    lane = lax.broadcasted_iota(jnp.int32, (size, size), 1)
    sub = lax.broadcasted_iota(jnp.int32, (size, size), 0)
    out[...] = jnp.where(lane <= sub, work[...], 0.0)


def inverse_factor(gram):
    return pl.pallas_call(
        factor_kernel,
        out_shape=jax.ShapeDtypeStruct(gram.shape, jnp.float32),
        in_specs=[pl.BlockSpec(memory_space=VMEM)],
        out_specs=pl.BlockSpec(memory_space=VMEM),
        scratch_shapes=[VMEM(gram.shape, jnp.float32)],
        compiler_params=pltpu.CompilerParams(vmem_limit_bytes=16 << 20),
    )(gram)


def white_kernel(text_scale, tag_scale, text, tag, inverses, text_out, tag_out):
    for panel, kind, out, scale in ((text, 0, text_out, text_scale), (tag, 1, tag_out, tag_scale)):
        whole = inverses[kind] * scale
        high = whole.astype(jnp.bfloat16)
        low = (whole - high.astype(jnp.float32)).astype(jnp.bfloat16)
        rows = panel.shape[0]
        step = min(rows, LANES)
        for at in range(0, rows, step):
            part = panel[at : at + step, :]
            dims = (((1,), (1,)), ((), ()))
            out[at : at + step, :] = lax.dot_general(
                part, high, dims, preferred_element_type=jnp.float32
            ) + lax.dot_general(part, low, dims, preferred_element_type=jnp.float32)


def whiten(text, tag, inverses, text_scale, tag_scale):
    return pl.pallas_call(
        functools.partial(white_kernel, text_scale, tag_scale),
        out_shape=(
            jax.ShapeDtypeStruct(text.shape, jnp.float32),
            jax.ShapeDtypeStruct(tag.shape, jnp.float32),
        ),
        in_specs=[pl.BlockSpec(memory_space=VMEM)] * 3,
        out_specs=[pl.BlockSpec(memory_space=VMEM)] * 2,
        compiler_params=pltpu.CompilerParams(vmem_limit_bytes=16 << 20),
    )(text, tag, inverses)


def local_gram(panel):
    return lax.dot_general(
        panel, panel, (((0,), (0,)), ((), ())), preferred_element_type=jnp.float32
    )


MESH = pl.DeviceIdType.MESH


def flip(me, offset):
    total, bit = me, 1
    while bit <= offset:
        if offset & bit:
            total = total + bit * (1 - 2 * lax.rem(lax.div(me, bit), 2))
        bit *= 2
    return total


def hypercube(size, rows, unit):
    bits = size.bit_length() - 1
    down = tuple(reversed(range(bits)))
    orders = [down]
    if bits >= 3:
        orders += [down[:-2] + (down[-1], down[-2]), (0, 1) + down[:-2]]
    units = rows // unit
    pieces, at = [], 0
    for number, order in enumerate(orders):
        here = units // len(orders) + (1 if number < units % len(orders) else 0)
        if here:
            pieces.append((order, at * unit, (at + here) * unit))
            at += here
    return pieces


def arrivals(order, stage):
    found = [1 << order[stage]]
    for bit in order[:stage]:
        found += [offset | 1 << bit for offset in found]
    return found


def greet(groups):
    barrier = pltpu.get_barrier_semaphore()
    for device in groups:
        pl.semaphore_signal(barrier, inc=1, device_id=device, device_id_type=MESH)
    pl.semaphore_wait(barrier, len(groups))


def tag_partners(size):
    me = lax.axis_index("tag")
    return [{"tag": flip(me, 1 << bit)} for bit in range(size.bit_length() - 1)]


def spread(pieces, source, place, send, recv):
    me = lax.axis_index("tag")
    copies = {}

    def go(number, offset, bit):
        order, lo, hi = pieces[number]
        owner = flip(me, offset)
        to = offset | 1 << bit
        copies[number, to] = pltpu.make_async_remote_copy(
            src_ref=source(lo, hi) if offset == 0 else place(owner, lo, hi),
            dst_ref=place(owner, lo, hi),
            send_sem=send.at[number, to],
            recv_sem=recv.at[number, to],
            device_id={"tag": flip(me, 1 << bit)},
            device_id_type=MESH,
        )
        copies[number, to].start()

    bits = len(pieces[0][0])
    for stage in range(bits):
        for number, (order, _, _) in enumerate(pieces):
            go(number, 0, order[stage])
    for stage in range(bits):
        for turn in range(1 << stage):
            for number, (order, _, _) in enumerate(pieces):
                offset = arrivals(order, stage)[turn]
                copies[number, offset].wait_recv()
                for later in range(stage + 1, bits):
                    go(number, offset, order[later])
    return copies


def collect_start(pieces, source, land, send, recv):
    me = lax.axis_index("tag")
    copies = {}
    last = len(pieces[0][0]) - 1
    for turn in range(1 << last):
        for number, (order, lo, hi) in enumerate(pieces):
            offset = arrivals(order, last)[turn]
            copies[number, offset] = pltpu.make_async_remote_copy(
                src_ref=source(flip(me, offset), lo, hi),
                dst_ref=land.at[offset, lo:hi],
                send_sem=send.at[number, offset],
                recv_sem=recv.at[number, offset],
                device_id={"tag": flip(me, 1 << order[last])},
                device_id_type=MESH,
            )
            copies[number, offset].start()
    return copies


def collect(pieces, copies, source, land, outgoing, finish, send, recv):
    me = lax.axis_index("tag")
    bits = len(pieces[0][0])

    def summed(number, offset, stage):
        order, lo, hi = pieces[number]
        total = source(flip(me, offset), lo, hi)[...].astype(jnp.float32)
        for later in reversed(range(stage + 1, bits)):
            come = offset | 1 << order[later]
            copies[number, come].wait_recv()
            total = total + land[come, lo:hi].astype(jnp.float32)
        return total

    for stage in reversed(range(bits - 1)):
        for turn in range(1 << stage):
            for number, (order, lo, hi) in enumerate(pieces):
                offset = arrivals(order, stage)[turn]
                outgoing[offset, lo:hi] = summed(number, offset, stage).astype(outgoing.dtype)
                copies[number, offset] = pltpu.make_async_remote_copy(
                    src_ref=outgoing.at[offset, lo:hi],
                    dst_ref=land.at[offset, lo:hi],
                    send_sem=send.at[number, offset],
                    recv_sem=recv.at[number, offset],
                    device_id={"tag": flip(me, 1 << order[stage])},
                    device_id_type=MESH,
                )
                copies[number, offset].start()
    for number, (_, lo, hi) in enumerate(pieces):
        finish(lo, hi, summed(number, 0, -1))


def drain(copies):
    for copy in copies.values():
        copy.wait_send()


def gather_kernel(size, pieces, shard, out, send, recv):
    rows = shard.shape[0]
    greet(tag_partners(size))

    def place(owner, lo, hi):
        return out.at[pl.ds(pl.multiple_of(owner * rows + lo, 16), hi - lo), :]

    copies = spread(pieces, lambda lo, hi: shard.at[lo:hi, :], place, send, recv)
    me = lax.axis_index("tag")
    out[pl.ds(pl.multiple_of(me * rows, 16), rows), :] = shard[...]
    drain(copies)


def remote_call(kernel, number, out_shape, scratch, count):
    many = isinstance(out_shape, tuple)
    spec = pl.BlockSpec(memory_space=VMEM)
    return pl.pallas_call(
        kernel,
        out_shape=out_shape,
        in_specs=[spec] * count,
        out_specs=[spec] * len(out_shape) if many else spec,
        scratch_shapes=scratch,
        cost_estimate=pl.CostEstimate(flops=0, bytes_accessed=50_000_000, transcendentals=0),
        compiler_params=pltpu.CompilerParams(
            collective_id=number, has_side_effects=True, vmem_limit_bytes=20 << 20
        ),
    )


def semaphores(*shape):
    return pltpu.SemaphoreType.DMA(shape)


def gather(shard, size):
    rows, comps = shard.shape
    pieces = hypercube(size, rows, 16)
    return remote_call(
        functools.partial(gather_kernel, size, pieces),
        0,
        jax.ShapeDtypeStruct((rows * size, comps), shard.dtype),
        [semaphores(len(pieces), size), semaphores(len(pieces), size)],
        1,
    )(shard)


def pair_sum_kernel(chunk, partial, out, mine, land, leaving, send, recv):
    core = lax.axis_index("text")
    sibling = {"text": 1 - core}
    half = mine.shape[0]
    greet([sibling])
    first, second = [], []
    for number in range(half // chunk):
        lo = number * chunk
        theirs = pl.multiple_of((1 - core) * half + lo, 16)
        leaving[lo : lo + chunk, :] = partial[pl.ds(theirs, chunk), :].astype(leaving.dtype)
        copy = pltpu.make_async_remote_copy(
            src_ref=leaving.at[lo : lo + chunk, :],
            dst_ref=land.at[lo : lo + chunk, :],
            send_sem=send.at[0, number],
            recv_sem=recv.at[0, number],
            device_id=sibling,
            device_id_type=MESH,
        )
        copy.start()
        first.append(copy)
    for number in range(half // chunk):
        lo = number * chunk
        ours = pl.ds(pl.multiple_of(core * half + lo, 16), chunk)
        first[number].wait_recv()
        total = (partial[ours, :] + land[lo : lo + chunk, :].astype(jnp.float32)).astype(out.dtype)
        mine[lo : lo + chunk, :] = total
        copy = pltpu.make_async_remote_copy(
            src_ref=mine.at[lo : lo + chunk, :],
            dst_ref=out.at[ours, :],
            send_sem=send.at[1, number],
            recv_sem=recv.at[1, number],
            device_id=sibling,
            device_id_type=MESH,
        )
        copy.start()
        second.append(copy)
        out[ours, :] = total
    for copy in first:
        copy.wait_send()
    for copy in second:
        copy.wait()


def pair_sum(partial):
    rows, comps = partial.shape
    half = rows // 2
    chunk = half // 6
    return remote_call(
        functools.partial(pair_sum_kernel, chunk),
        1,
        (
            jax.ShapeDtypeStruct((rows, comps), jnp.bfloat16),
            jax.ShapeDtypeStruct((half, comps), jnp.bfloat16),
        ),
        [
            VMEM((half, comps), jnp.bfloat16),
            VMEM((half, comps), jnp.bfloat16),
            semaphores(2, 6),
            semaphores(2, 6),
        ],
        1,
    )(partial)


def scatter_kernel(size, pieces, partial, out, land, outgoing, send, recv):
    rows = out.shape[0]
    greet(tag_partners(size))

    def source(owner, lo, hi):
        return partial.at[pl.ds(pl.multiple_of(owner * rows + lo, 16), hi - lo), :]

    def finish(lo, hi, total):
        out[lo:hi, :] = total.astype(out.dtype)

    copies = collect_start(pieces, source, land, send, recv)
    collect(pieces, copies, source, land, outgoing, finish, send, recv)
    drain(copies)


def scatter_sum(partial, size):
    rows, comps = partial.shape[0] // size, partial.shape[1]
    pieces = hypercube(size, rows, 16)
    return remote_call(
        functools.partial(scatter_kernel, size, pieces),
        2,
        jax.ShapeDtypeStruct((rows, comps), jnp.bfloat16),
        [
            VMEM((size, rows, comps), jnp.bfloat16),
            VMEM((size, rows, comps), jnp.bfloat16),
            semaphores(len(pieces), size),
            semaphores(len(pieces), size),
        ],
        1,
    )(partial)


def lower(blocks):
    return [(i, j) for i in range(blocks) for j in range(i + 1)]


def gram_kernel(size, pieces, text, tag, out, both, other, own, gathered, land, outgoing, pair, sems):
    core = lax.axis_index("text")
    me = lax.axis_index("tag")
    rows = own.shape[1]
    pairs = lower(out.shape[0] // LANES)
    sibling = {"text": 1 - core}
    greet(tag_partners(size) + [sibling])
    for kind, panel in ((0, text), (1, tag)):
        gram = local_gram(panel[...])
        for at, (i, j) in enumerate(pairs):
            both[kind, at] = gram[i * LANES : (i + 1) * LANES, j * LANES : (j + 1) * LANES]
    swap = pltpu.make_async_remote_copy(
        src_ref=both.at[1 - core],
        dst_ref=other,
        send_sem=pair.at[0],
        recv_sem=pair.at[1],
        device_id=sibling,
        device_id_type=MESH,
    )
    swap.start()
    swap.wait()
    other[...] += both[core]

    def place(owner, lo, hi):
        return gathered.at[lo:hi, pl.ds(pl.multiple_of(owner * rows, 8), rows), :]

    def source(owner, lo, hi):
        return other.at[lo:hi, pl.ds(pl.multiple_of(owner * rows, 8), rows), :]

    def finish(lo, hi, total):
        own[lo:hi] = total

    copies = collect_start(pieces, source, land, sems.at[0], sems.at[1])
    collect(pieces, copies, source, land, outgoing, finish, sems.at[0], sems.at[1])
    more = spread(pieces, lambda lo, hi: own.at[lo:hi], place, sems.at[2], sems.at[3])
    gathered[:, pl.ds(pl.multiple_of(me * rows, 8), rows), :] = own[...]
    drain(copies)
    drain(more)
    for at, (i, j) in enumerate(pairs):
        block = gathered[at]
        if i == j:
            out[i * LANES : (i + 1) * LANES, j * LANES : (j + 1) * LANES] = block
        else:
            out[j * LANES : (j + 1) * LANES, i * LANES : (i + 1) * LANES] = block.T
            out[i * LANES : (i + 1) * LANES, j * LANES : (j + 1) * LANES] = block


def gram_sum(text, tag, size):
    comps = text.shape[1]
    rows = LANES // size
    count = len(lower(comps // LANES))
    pieces = hypercube(size, count, 1)
    square = jax.ShapeDtypeStruct((comps, comps), jnp.float32)
    return remote_call(
        functools.partial(gram_kernel, size, pieces),
        3,
        square,
        [
            VMEM((2, count, LANES, LANES), jnp.float32),
            VMEM((count, LANES, LANES), jnp.float32),
            VMEM((count, rows, LANES), jnp.float32),
            VMEM((count, LANES, LANES), jnp.float32),
            VMEM((size, count, rows, LANES), jnp.float32),
            VMEM((size, count, rows, LANES), jnp.float32),
            semaphores(2),
            semaphores(4, len(pieces), size),
        ],
        2,
    )(text, tag)


def swap_kernel(inverse, out, sems):
    core = lax.axis_index("text")
    sibling = {"text": 1 - core}
    greet([sibling])
    swap = pltpu.make_async_remote_copy(
        src_ref=inverse,
        dst_ref=out.at[core],
        send_sem=sems.at[0],
        recv_sem=sems.at[1],
        device_id=sibling,
        device_id_type=MESH,
    )
    swap.start()
    out[core] = inverse[...]
    swap.wait()


def swap_inverses(inverse):
    return remote_call(
        swap_kernel,
        4,
        jax.ShapeDtypeStruct((2,) + inverse.shape, jnp.float32),
        [semaphores(2)],
        1,
    )(inverse)


def shards(tile_values, tile_rows, tile_cols, tile_counts, panel_init):
    tiles = tile_values[0]
    rows = tile_rows[0]
    cols = tile_cols[0]
    count = tile_counts[0]
    width = tiles.shape[1]
    comps = panel_init.shape[1]
    text_size = lax.axis_size("text")
    tag_size = lax.axis_size("tag")
    column_span = TC * width
    share = column_span // text_size
    paired = text_size == 2 and LANES // tag_size >= 8
    row_block = gather(panel_init, tag_size)
    row_span = row_block.shape[0]

    tag_partial = tile_product(
        tag_kernel, tiles, rows, cols, count, row_block, column_span, jnp.float32, []
    )
    if paired:
        column_block, tag_mine = pair_sum(tag_partial)
    else:
        column_block = lax.psum(tag_partial, "text").astype(jnp.bfloat16)
        tag_mine = lax.dynamic_slice_in_dim(
            column_block, lax.axis_index("text") * share, share, 0
        )
    text_partial = tile_product(
        text_kernel,
        tiles,
        rows,
        cols,
        count,
        column_block,
        row_span,
        jnp.bfloat16,
        [VMEM((row_span, comps), jnp.float32)],
    )
    text_mine = scatter_sum(text_partial, tag_size)
    if paired:
        gram = gram_sum(text_mine, tag_mine, tag_size)
        inverses = swap_inverses(inverse_factor(gram))
    else:
        text_gram, tag_gram = lax.psum(
            (local_gram(text_mine), local_gram(tag_mine)), ("text", "tag")
        )
        inverses = jnp.stack([inverse_factor(text_gram), inverse_factor(tag_gram)])
    text_total = text_mine.shape[0] * tag_size * text_size
    tag_total = column_span * tag_size
    return whiten(text_mine, tag_mine, inverses, math.sqrt(text_total), math.sqrt(tag_total))


def solution(mesh):
    in_specs = (
        P("text", "tag", None, None),
        P("text", "tag"),
        P("text", "tag"),
        P("text", "tag"),
        P(("text", "tag"), None),
    )
    out_specs = (P(("text", "tag"), None), P(("tag", "text"), None))
    return jax.shard_map(shards, mesh=mesh, in_specs=in_specs, out_specs=out_specs, check_vma=False)
```

profile of v0, /device:TPU:0, one launch (start us, length us, event | category | flops | bytes accessed | tf_op | source)
XLA Modules:
  0.0 130.3 jit_solution(2721557743119125726)
XLA Ops:
  0.6 0.0 copy-start.4
  0.6 0.0 copy-start.3
  1.3 0.0 copy-start.2
  1.3 0.9 copy-done.2
  2.2 24.8 %shard_map.68.panel = bf16[2048,512]{1,0:T(8,128)(2,1)S(1)} custom-call(bf16[128,512]{1,0:T(8,128)(2,1)S(1)} %copy-done.2), custom_call_target="tpu_custom_call" | custom-call | bytes 50000000 | tf_op jit(solution)/shard_map/pallas_call | solution.py:374
  27.1 0.0 copy-done.4
  27.1 0.0 copy-done.3
  27.1 0.0 copy-start
  27.1 2.5 %copy-done = bf16[1,10,512,512]{3,2,1,0:T(8,128)(2,1)S(1)} copy-done((bf16[1,10,512,512]{3,2,1,0:T(8,128)(2,1)S(1)}, bf16[1,10,512,512]{3,2,1,0:T(8,128)(2,1)}, u32[]{:S(2)}) %copy-start) | copy-done | bytes 5242904
  29.6 0.0 copy-start.1
  29.6 5.2 %shard_map.69.partial = f32[1536,512]{1,0:T(8,128)S(1)} custom-call(s32[10]{0:T(128)S(1)} %bitcast.8, s32[10]{0:T(128)S(1)} %bitcast.10, s32[1]{0:T(128)} %bitcast.4.count, bf16[10,512,512]{2,1,0:T(8,128)(2,1)S(1)} %bitcast.6, bf16[2048,512]{1,0:T(8,128)(2,1)S(1)} %shard_map.68.panel), custom_call_target="tpu_custom_call" | custom-call | tf_op jit(solution)/shard_map/pallas_call | solution.py:62
  34.7 3.7 %shard_map.70 = (bf16[1536,512]{1,0:T(8,128)(2,1)S(1)}, bf16[768,512]{1,0:T(8,128)(2,1)S(1)}) custom-call(f32[1536,512]{1,0:T(8,128)S(1)} %shard_map.69.partial), custom_call_target="tpu_custom_call" | custom-call | bytes 50000000 | tf_op jit(solution)/shard_map/pallas_call | solution.py:430
  38.4 0.0 copy-done.1
  38.4 5.4 %shard_map.71.partial = bf16[2048,512]{1,0:T(8,128)(2,1)S(1)} custom-call(s32[10]{0:T(128)S(1)} %bitcast.9, s32[10]{0:T(128)S(1)} %bitcast.11, s32[1]{0:T(128)} %bitcast.5.count, bf16[10,512,512]{2,1,0:T(8,128)(2,1)S(1)} %bitcast.7, bf16[1536,512]{1,0:T(8,128)(2,1)S(1)} %get-tuple-element.4.panel), custom_call_target="tpu_custom_call" | custom-call | tf_op jit(solution)/shard_map/pallas_call | solution.py:62
  43.9 26.0 %shard_map.72.text = bf16[128,512]{1,0:T(8,128)(2,1)S(1)} custom-call(bf16[2048,512]{1,0:T(8,128)(2,1)S(1)} %shard_map.71.partial), custom_call_target="tpu_custom_call" | custom-call | bytes 50000000 | tf_op jit(solution)/shard_map/pallas_call | solution.py:465
  69.9 32.7 %shard_map.73.gram = f32[512,512]{1,0:T(8,128)S(1)} custom-call(bf16[128,512]{1,0:T(8,128)(2,1)S(1)} %shard_map.72.text, bf16[768,512]{1,0:T(8,128)(2,1)S(1)} %get-tuple-element.5.tag), custom_call_target="tpu_custom_call" | custom-call | bytes 50000000 | tf_op jit(solution)/shard_map/pallas_call | solution.py:536
  102.6 21.3 %shard_map.74.inverse = f32[512,512]{1,0:T(8,128)S(1)} custom-call(f32[512,512]{1,0:T(8,128)S(1)} %shard_map.73.gram), custom_call_target="tpu_custom_call" | custom-call | tf_op jit(solution)/shard_map/pallas_call | solution.py:160
  123.9 2.7 %shard_map.75.inverses = f32[2,512,512]{2,1,0:T(8,128)S(1)} custom-call(f32[512,512]{1,0:T(8,128)S(1)} %shard_map.74.inverse), custom_call_target="tpu_custom_call" | custom-call | bytes 50000000 | tf_op jit(solution)/shard_map/pallas_call | solution.py:572
  126.6 3.7 %shard_map.76 = (f32[128,512]{1,0:T(8,128)}, f32[768,512]{1,0:T(8,128)}) custom-call(bf16[128,512]{1,0:T(8,128)(2,1)S(1)} %shard_map.72.text, bf16[768,512]{1,0:T(8,128)(2,1)S(1)} %get-tuple-element.5.tag, f32[2,512,512]{2,1,0:T(8,128)S(1)} %shard_map.75.inverses), custom_call_target="tpu_custom_call" | custom-call | tf_op jit(solution)/shard_map/pallas_call | solution.py:186
Async XLA Ops:
  0.6 26.4 %copy-start.4 = (s32[1,10]{1,0:T(1,128)S(1)}, s32[1,10]{1,0:T(1,128)}, u32[]{:S(2)}) copy-start(s32[1,10]{1,0:T(1,128)} %param.7) | copy-start | bytes 124
  0.6 26.4 %copy-start.3 = (s32[1,10]{1,0:T(1,128)S(1)}, s32[1,10]{1,0:T(1,128)}, u32[]{:S(2)}) copy-start(s32[1,10]{1,0:T(1,128)} %param.6) | copy-start | bytes 124
  1.3 0.9 copy-start.2
  27.1 2.5 %copy-start = (bf16[1,10,512,512]{3,2,1,0:T(8,128)(2,1)S(1)}, bf16[1,10,512,512]{3,2,1,0:T(8,128)(2,1)}, u32[]{:S(2)}) copy-start(bf16[1,10,512,512]{3,2,1,0:T(8,128)(2,1)} %param.5) | copy-start | bytes 15728644
  29.6 8.8 %copy-start.1 = (bf16[1,10,512,512]{3,2,1,0:T(8,128)(2,1)S(1)}, bf16[1,10,512,512]{3,2,1,0:T(8,128)(2,1)}, u32[]{:S(2)}) copy-start(bf16[1,10,512,512]{3,2,1,0:T(8,128)(2,1)} %param.5) | copy-start | bytes 15728644
where the time goes:
time: 130 us
  Pallas kernels  125 us (96%)
  local copies, waits for them, and re-layouts  3.39 us (3%)
  between operations  1.42 us (1%)
    pallas_call x1, Pallas kernels, gram_sum(): remote_call(functools.partial(gram_kernel, size, pieces), 3, square, [VME...  32.7 us
    pallas_call x1, Pallas kernels, scatter_sum(): remote_call(functools.partial(scatter_kernel, size, pieces), 2, jax.Shape...  26 us
    pallas_call x1, Pallas kernels, gather(): remote_call(functools.partial(gather_kernel, size, pieces), 0, jax.ShapeD...  24.8 us
    pallas_call x1, Pallas kernels, inverse_factor(): pl.pallas_call(factor_kernel, out_shape=jax.ShapeDtypeStruct(gram.shape,...  21.3 us
    pallas_call x2, Pallas kernels, tile_product(): pl.pallas_call(kernel, out_shape=jax.ShapeDtypeStruct((out_rows, comps),...  10.6 us
    pallas_call x1, Pallas kernels, pair_sum(): remote_call(functools.partial(pair_sum_kernel, chunk), 1, (jax.ShapeDtype...  3.67 us
    pallas_call x1, Pallas kernels, whiten(): pl.pallas_call(functools.partial(white_kernel, text_scale, tag_scale), ou...  3.66 us
    unnamed x10, local copies, waits for them, and re-layouts  3.39 us

commit v1 on v0

--- a/solution.py
+++ b/solution.py
@@ -81,6 +81,7 @@
     groups = size // 8
     lane = lax.broadcasted_iota(jnp.int32, (8, size), 1)
     sub = lax.broadcasted_iota(jnp.int32, (8, size), 0)
+    fixed = [jnp.full((8, size), s, jnp.int32) for s in range(8)]
     m = [block[8 * g : 8 * g + 8, :] for g in range(groups)]
     pivots = []
 
@@ -89,38 +90,55 @@
 
     def down(rows, s):
         return jnp.broadcast_to(rows[s : s + 1, :], (8, size))
+
+    def splat(rows, s):
+        return jnp.take_along_axis(rows, fixed[s], axis=0, mode="promise_in_bounds")
 
     for g in range(groups):
         at = 8 * g
         inside = (lane >= at) & (lane < at + 8)
         own = [across(m[g], at + t) for t in range(8)]
-        entry = {(s, t): down(own[t], s) for t in range(8) for s in range(t, 8)}
+        entry = {(s, t): splat(own[t], s) for t in range(8) for s in range(t, 8)}
         start = jnp.where(inside, jnp.where(lane == sub + at, 1.0, 0.0), m[g])
         rows = [down(start, s) for s in range(8)]
-        ratio, inverse, scaled = {}, [], []
-        for t in range(8):
-            inverse.append(1.0 / entry[t, t])
-            for s in range(t + 1, 8):
-                ratio[s, t] = entry[s, t] * inverse[t]
-            for q in range(t + 1, 8):
+        pivot, steps = [None] * 8, []
+        for t in range(0, 8, 2):
+            a, b, c = entry[t, t], entry[t + 1, t], entry[t + 1, t + 1]
+            det = a * c - b * b
+            inverse, first = 1.0 / det, 1.0 / a
+            later = range(t + 2, 8)
+            left = {q: c * entry[q, t] - b * entry[q, t + 1] for q in later}
+            right = {q: a * entry[q, t + 1] - b * entry[q, t] for q in later}
+            for q in later:
                 for s in range(q, 8):
-                    entry[s, q] = entry[s, q] - ratio[q, t] * entry[s, t]
-                rows[q] = rows[q] - ratio[q, t] * rows[t]
-            scaled.append(rows[t] * inverse[t])
+                    taken = left[q] * entry[s, t] + right[q] * entry[s, t + 1]
+                    entry[s, q] = entry[s, q] - inverse * taken
+            left = {q: inverse * left[q] for q in later}
+            right = {q: inverse * right[q] for q in later}
+            upper, under = rows[t], rows[t + 1]
+            for q in later:
+                rows[q] = rows[q] - (left[q] * upper + right[q] * under)
+            steps.append(
+                (left, right, inverse * (c * upper - b * under), inverse * (a * under - b * upper))
+            )
+            rows[t + 1] = under - (b * first) * upper
+            pivot[t], pivot[t + 1] = a, det * first
         for i in range(g + 1, groups):
             columns = [across(m[i], at + t) for t in range(8)]
             total = jnp.where(inside, 0.0, m[i])
-            for t in range(8):
-                for q in range(t + 1, 8):
-                    columns[q] = columns[q] - ratio[q, t] * columns[t]
-                total = total - columns[t] * scaled[t]
+            for t in range(0, 8, 2):
+                left, right, upper, under = steps[t // 2]
+                for q in range(t + 2, 8):
+                    taken = left[q] * columns[t] + right[q] * columns[t + 1]
+                    columns[q] = columns[q] - taken
+                total = total - (columns[t] * upper + columns[t + 1] * under)
             m[i] = total
-        done, pivot = rows[0], entry[0, 0]
+        done, kept = rows[0], pivot[0]
         for t in range(1, 8):
             done = jnp.where(sub == t, rows[t], done)
-            pivot = jnp.where(sub == t, entry[t, t], pivot)
+            kept = jnp.where(sub == t, pivot[t], kept)
         m[g] = done
-        pivots.append(pivot)
+        pivots.append(kept)
     out = []
     for g in range(groups):
         kept = jnp.where(lane <= sub + 8 * g, m[g], 0.0)
@@ -128,11 +146,21 @@
     return jnp.concatenate(out, axis=0)
 
 
-def factor_kernel(gram, out, work):
-    size = gram.shape[0]
+def factor_in_place(work, scale, out):
+    size = work.shape[0]
     blocks = size // LANES
-    work[...] = gram[...]
     exact = lax.Precision.HIGHEST
+    lane = lax.broadcasted_iota(jnp.int32, (LANES, LANES), 1)
+    sub = lax.broadcasted_iota(jnp.int32, (LANES, LANES), 0)
+    tall = []
+    for b in range(blocks):
+        lo, hi = b * LANES, (b + 1) * LANES
+        diagonal = jnp.where(lane == sub, work[lo:hi, lo:hi], 0.0)
+        scale[:, lo:hi] = lax.rsqrt(jnp.sum(diagonal, axis=0, keepdims=True))
+        tall.append(lax.rsqrt(jnp.sum(diagonal, axis=1, keepdims=True)))
+    for b in range(blocks):
+        lo, hi = b * LANES, (b + 1) * LANES
+        work[lo:hi, :] = (work[lo:hi, :] * tall[b]) * scale[...]
 
     for b in range(blocks):
         lo, hi = b * LANES, (b + 1) * LANES
@@ -151,9 +179,14 @@
                 preferred_element_type=jnp.float32,
                 precision=exact,
             )
-    lane = lax.broadcasted_iota(jnp.int32, (size, size), 1)
-    sub = lax.broadcasted_iota(jnp.int32, (size, size), 0)
-    out[...] = jnp.where(lane <= sub, work[...], 0.0)
+        lanes = lax.broadcasted_iota(jnp.int32, (LANES, size), 1)
+        subs = lax.broadcasted_iota(jnp.int32, (LANES, size), 0) + lo
+        out[lo:hi, :] = jnp.where(lanes <= subs, work[lo:hi, :] * scale[...], 0.0)
+
+
+def factor_kernel(gram, out, work, scale):
+    work[...] = gram[...]
+    factor_in_place(work, scale, out)
 
 
 def inverse_factor(gram):
@@ -162,7 +195,7 @@
         out_shape=jax.ShapeDtypeStruct(gram.shape, jnp.float32),
         in_specs=[pl.BlockSpec(memory_space=VMEM)],
         out_specs=pl.BlockSpec(memory_space=VMEM),
-        scratch_shapes=[VMEM(gram.shape, jnp.float32)],
+        scratch_shapes=[VMEM(gram.shape, jnp.float32), VMEM((1, gram.shape[1]), jnp.float32)],
         compiler_params=pltpu.CompilerParams(vmem_limit_bytes=16 << 20),
     )(gram)
 

time: 130 us -> 123 us (0.946)
  Pallas kernels: 125 us -> 117 us
    pallas_call x1, Pallas kernels: 21.3 us -> 13.9 us  [inverse_factor(): pl.pallas_call(factor_kernel, out_shape=jax.ShapeDtypeStruct(gram.shape,...]
where the time goes in v1:
time: 123 us; the launch traced here: 122 us
  Pallas kernels  117 us (95%)
  local copies, waits for them, and re-layouts  3.39 us (3%)
  between operations  1.42 us (1%)
    pallas_call x1, Pallas kernels, gram_sum(): remote_call(functools.partial(gram_kernel, size, pieces), 3, square, [VME...  31.4 us
    pallas_call x1, Pallas kernels, scatter_sum(): remote_call(functools.partial(scatter_kernel, size, pieces), 2, jax.Shape...  25.8 us
    pallas_call x1, Pallas kernels, gather(): remote_call(functools.partial(gather_kernel, size, pieces), 0, jax.ShapeD...  24.8 us
    pallas_call x1, Pallas kernels, inverse_factor(): pl.pallas_call(factor_kernel, out_shape=jax.ShapeDtypeStruct(gram.shape,...  13.9 us
    pallas_call x2, Pallas kernels, tile_product(): pl.pallas_call(kernel, out_shape=jax.ShapeDtypeStruct((out_rows, comps),...  11.5 us
    pallas_call x1, Pallas kernels, pair_sum(): remote_call(functools.partial(pair_sum_kernel, chunk), 1, (jax.ShapeDtype...  3.67 us
    pallas_call x1, Pallas kernels, whiten(): pl.pallas_call(functools.partial(white_kernel, text_scale, tag_scale), ou...  3.66 us
    unnamed x10, local copies, waits for them, and re-layouts  3.39 us

profile of v1, /device:TPU:0, one launch (start us, length us, event | category | flops | bytes accessed | tf_op | source)
XLA Modules:
  0.0 122.3 jit_solution(7029504451650556156)
XLA Ops:
  0.6 0.0 copy-start.4
  0.6 0.0 copy-start.3
  1.3 0.0 copy-start.2
  1.3 0.9 copy-done.2
  2.2 24.8 %shard_map.68.panel = bf16[2048,512]{1,0:T(8,128)(2,1)S(1)} custom-call(bf16[128,512]{1,0:T(8,128)(2,1)S(1)} %copy-done.2), custom_call_target="tpu_custom_call" | custom-call | bytes 50000000 | tf_op jit(solution)/shard_map/pallas_call | solution.py:407
  27.1 0.0 copy-done.4
  27.1 0.0 copy-done.3
  27.1 0.0 copy-start
  27.1 2.5 %copy-done = bf16[1,10,512,512]{3,2,1,0:T(8,128)(2,1)S(1)} copy-done((bf16[1,10,512,512]{3,2,1,0:T(8,128)(2,1)S(1)}, bf16[1,10,512,512]{3,2,1,0:T(8,128)(2,1)}, u32[]{:S(2)}) %copy-start) | copy-done | bytes 5242904
  29.6 0.0 copy-start.1
  29.6 5.6 %shard_map.69.partial = f32[1536,512]{1,0:T(8,128)S(1)} custom-call(s32[10]{0:T(128)S(1)} %bitcast.8, s32[10]{0:T(128)S(1)} %bitcast.10, s32[1]{0:T(128)} %bitcast.4.count, bf16[10,512,512]{2,1,0:T(8,128)(2,1)S(1)} %bitcast.6, bf16[2048,512]{1,0:T(8,128)(2,1)S(1)} %shard_map.68.panel), custom_call_target="tpu_custom_call" | custom-call | tf_op jit(solution)/shard_map/pallas_call | solution.py:62
  35.2 3.7 %shard_map.70 = (bf16[1536,512]{1,0:T(8,128)(2,1)S(1)}, bf16[768,512]{1,0:T(8,128)(2,1)S(1)}) custom-call(f32[1536,512]{1,0:T(8,128)S(1)} %shard_map.69.partial), custom_call_target="tpu_custom_call" | custom-call | bytes 50000000 | tf_op jit(solution)/shard_map/pallas_call | solution.py:463
  38.9 0.0 copy-done.1
  38.9 5.8 %shard_map.71.partial = bf16[2048,512]{1,0:T(8,128)(2,1)S(1)} custom-call(s32[10]{0:T(128)S(1)} %bitcast.9, s32[10]{0:T(128)S(1)} %bitcast.11, s32[1]{0:T(128)} %bitcast.5.count, bf16[10,512,512]{2,1,0:T(8,128)(2,1)S(1)} %bitcast.7, bf16[1536,512]{1,0:T(8,128)(2,1)S(1)} %get-tuple-element.4.panel), custom_call_target="tpu_custom_call" | custom-call | tf_op jit(solution)/shard_map/pallas_call | solution.py:62
  44.7 25.8 %shard_map.72.text = bf16[128,512]{1,0:T(8,128)(2,1)S(1)} custom-call(bf16[2048,512]{1,0:T(8,128)(2,1)S(1)} %shard_map.71.partial), custom_call_target="tpu_custom_call" | custom-call | bytes 50000000 | tf_op jit(solution)/shard_map/pallas_call | solution.py:498
  70.5 31.4 %shard_map.73.gram = f32[512,512]{1,0:T(8,128)S(1)} custom-call(bf16[128,512]{1,0:T(8,128)(2,1)S(1)} %shard_map.72.text, bf16[768,512]{1,0:T(8,128)(2,1)S(1)} %get-tuple-element.5.tag), custom_call_target="tpu_custom_call" | custom-call | bytes 50000000 | tf_op jit(solution)/shard_map/pallas_call | solution.py:569
  102.0 13.9 %shard_map.74.inverse = f32[512,512]{1,0:T(8,128)S(1)} custom-call(f32[512,512]{1,0:T(8,128)S(1)} %shard_map.73.gram), custom_call_target="tpu_custom_call" | custom-call | tf_op jit(solution)/shard_map/pallas_call | solution.py:193
  115.9 2.7 %shard_map.75.inverses = f32[2,512,512]{2,1,0:T(8,128)S(1)} custom-call(f32[512,512]{1,0:T(8,128)S(1)} %shard_map.74.inverse), custom_call_target="tpu_custom_call" | custom-call | bytes 50000000 | tf_op jit(solution)/shard_map/pallas_call | solution.py:605
  118.6 3.7 %shard_map.76 = (f32[128,512]{1,0:T(8,128)}, f32[768,512]{1,0:T(8,128)}) custom-call(bf16[128,512]{1,0:T(8,128)(2,1)S(1)} %shard_map.72.text, bf16[768,512]{1,0:T(8,128)(2,1)S(1)} %get-tuple-element.5.tag, f32[2,512,512]{2,1,0:T(8,128)S(1)} %shard_map.75.inverses), custom_call_target="tpu_custom_call" | custom-call | tf_op jit(solution)/shard_map/pallas_call | solution.py:219
Async XLA Ops:
  0.6 26.4 %copy-start.4 = (s32[1,10]{1,0:T(1,128)S(1)}, s32[1,10]{1,0:T(1,128)}, u32[]{:S(2)}) copy-start(s32[1,10]{1,0:T(1,128)} %param.7) | copy-start | bytes 124
  0.6 26.4 %copy-start.3 = (s32[1,10]{1,0:T(1,128)S(1)}, s32[1,10]{1,0:T(1,128)}, u32[]{:S(2)}) copy-start(s32[1,10]{1,0:T(1,128)} %param.6) | copy-start | bytes 124
  1.3 0.9 copy-start.2
  27.1 2.5 %copy-start = (bf16[1,10,512,512]{3,2,1,0:T(8,128)(2,1)S(1)}, bf16[1,10,512,512]{3,2,1,0:T(8,128)(2,1)}, u32[]{:S(2)}) copy-start(bf16[1,10,512,512]{3,2,1,0:T(8,128)(2,1)} %param.5) | copy-start | bytes 15728644
  29.6 9.3 %copy-start.1 = (bf16[1,10,512,512]{3,2,1,0:T(8,128)(2,1)S(1)}, bf16[1,10,512,512]{3,2,1,0:T(8,128)(2,1)}, u32[]{:S(2)}) copy-start(bf16[1,10,512,512]{3,2,1,0:T(8,128)(2,1)} %param.5) | copy-start | bytes 15728644

commit v2 on v1

--- a/solution.py
+++ b/solution.py
@@ -413,70 +413,6 @@
     )(shard)
 
 
-def pair_sum_kernel(chunk, partial, out, mine, land, leaving, send, recv):
-    core = lax.axis_index("text")
-    sibling = {"text": 1 - core}
-    half = mine.shape[0]
-    greet([sibling])
-    first, second = [], []
-    for number in range(half // chunk):
-        lo = number * chunk
-        theirs = pl.multiple_of((1 - core) * half + lo, 16)
-        leaving[lo : lo + chunk, :] = partial[pl.ds(theirs, chunk), :].astype(leaving.dtype)
-        copy = pltpu.make_async_remote_copy(
-            src_ref=leaving.at[lo : lo + chunk, :],
-            dst_ref=land.at[lo : lo + chunk, :],
-            send_sem=send.at[0, number],
-            recv_sem=recv.at[0, number],
-            device_id=sibling,
-            device_id_type=MESH,
-        )
-        copy.start()
-        first.append(copy)
-    for number in range(half // chunk):
-        lo = number * chunk
-        ours = pl.ds(pl.multiple_of(core * half + lo, 16), chunk)
-        first[number].wait_recv()
-        total = (partial[ours, :] + land[lo : lo + chunk, :].astype(jnp.float32)).astype(out.dtype)
-        mine[lo : lo + chunk, :] = total
-        copy = pltpu.make_async_remote_copy(
-            src_ref=mine.at[lo : lo + chunk, :],
-            dst_ref=out.at[ours, :],
-            send_sem=send.at[1, number],
-            recv_sem=recv.at[1, number],
-            device_id=sibling,
-            device_id_type=MESH,
-        )
-        copy.start()
-        second.append(copy)
-        out[ours, :] = total
-    for copy in first:
-        copy.wait_send()
-    for copy in second:
-        copy.wait()
-
-
-def pair_sum(partial):
-    rows, comps = partial.shape
-    half = rows // 2
-    chunk = half // 6
-    return remote_call(
-        functools.partial(pair_sum_kernel, chunk),
-        1,
-        (
-            jax.ShapeDtypeStruct((rows, comps), jnp.bfloat16),
-            jax.ShapeDtypeStruct((half, comps), jnp.bfloat16),
-        ),
-        [
-            VMEM((half, comps), jnp.bfloat16),
-            VMEM((half, comps), jnp.bfloat16),
-            semaphores(2, 6),
-            semaphores(2, 6),
-        ],
-        1,
-    )(partial)
-
-
 def scatter_kernel(size, pieces, partial, out, land, outgoing, send, recv):
     rows = out.shape[0]
     greet(tag_partners(size))
@@ -507,6 +443,287 @@
         ],
         1,
     )(partial)
+
+
+def spread_steps(pieces, source, place, send, recv, copies):
+    me = lax.axis_index("tag")
+
+    def go(number, offset, bit):
+        order, lo, hi = pieces[number]
+        owner = flip(me, offset)
+        to = offset | 1 << bit
+        copies[number, to] = pltpu.make_async_remote_copy(
+            src_ref=source(lo, hi) if offset == 0 else place(owner, lo, hi),
+            dst_ref=place(owner, lo, hi),
+            send_sem=send.at[number, to],
+            recv_sem=recv.at[number, to],
+            device_id={"tag": flip(me, 1 << bit)},
+            device_id_type=MESH,
+        )
+        copies[number, to].start()
+
+    bits = len(pieces[0][0])
+    for stage in range(bits):
+        for number, (order, _, _) in enumerate(pieces):
+            go(number, 0, order[stage])
+    yield
+    for stage in range(bits):
+        for turn in range(1 << stage):
+            for number, (order, _, _) in enumerate(pieces):
+                offset = arrivals(order, stage)[turn]
+                copies[number, offset].wait_recv()
+                for later in range(stage + 1, bits):
+                    go(number, offset, order[later])
+                yield
+
+
+def collect_steps(pieces, source, land, outgoing, finish, send, recv, copies):
+    me = lax.axis_index("tag")
+    bits = len(pieces[0][0])
+
+    def go(number, offset, bit, ref):
+        _, lo, hi = pieces[number]
+        copies[number, offset] = pltpu.make_async_remote_copy(
+            src_ref=ref,
+            dst_ref=land(offset, lo, hi),
+            send_sem=send.at[number, offset],
+            recv_sem=recv.at[number, offset],
+            device_id={"tag": flip(me, 1 << bit)},
+            device_id_type=MESH,
+        )
+        copies[number, offset].start()
+
+    def summed(number, offset, stage):
+        order, lo, hi = pieces[number]
+        total = source(flip(me, offset), lo, hi)[...].astype(jnp.float32)
+        for later in reversed(range(stage + 1, bits)):
+            come = offset | 1 << order[later]
+            copies[number, come].wait_recv()
+            total = total + land(come, lo, hi)[...].astype(jnp.float32)
+        return total
+
+    last = bits - 1
+    for turn in reversed(range(1 << last)):
+        for number, (order, lo, hi) in enumerate(pieces):
+            offset = arrivals(order, last)[turn]
+            go(number, offset, order[last], source(flip(me, offset), lo, hi))
+    yield
+    for stage in reversed(range(last)):
+        for turn in reversed(range(1 << stage)):
+            for number, (order, lo, hi) in enumerate(pieces):
+                offset = arrivals(order, stage)[turn]
+                leaving = outgoing(offset, lo, hi)
+                leaving[...] = summed(number, offset, stage).astype(leaving.dtype)
+                go(number, offset, order[stage], leaving)
+                yield
+    for number, (_, lo, hi) in enumerate(pieces):
+        finish(lo, hi, summed(number, 0, -1))
+        yield
+
+
+def advance(steps, count):
+    for _ in range(count):
+        if next(steps, steps) is steps:
+            return False
+    return True
+
+
+def finish_steps(steps):
+    for _ in steps:
+        pass
+
+
+def weave(work, steps, lead, ratio):
+    for number, _ in enumerate(work):
+        if number >= lead:
+            advance(steps, ratio)
+
+
+def front_kernel(
+    size, pieces, shard, stored, tile_rows, tile_cols, tile_counts, text_out, tag_out,
+    tiles, table, panel, total, leaving, arrived, columns, partial, land, outgoing,
+    tile_sem, gather_sems, pair_sems, scatter_sems,
+):
+    core = lax.axis_index("text")
+    me = lax.axis_index("tag")
+    sibling = {"text": 1 - core}
+    slots, width, _ = stored.shape
+    rows = shard.shape[0]
+    parts, row_span, part = panel.shape
+    column_span = columns.shape[1]
+    row_tiles, column_tiles = row_span // width, column_span // width
+    half = column_span // 2
+    chunk = half // column_tiles
+    load = pltpu.make_async_copy(stored, tiles.at[0:slots], tile_sem)
+    load.start()
+    greet(tag_partners(size) + [sibling])
+
+    def lanes(h):
+        return slice(h * part, (h + 1) * part)
+
+    def gather(h, copies):
+        def place(owner, lo, hi):
+            return panel.at[h, pl.ds(pl.multiple_of(owner * rows + lo, 16), hi - lo), :]
+
+        def source(lo, hi):
+            return shard.at[lo:hi, lanes(h)]
+
+        sems = gather_sems
+        return spread_steps(pieces, source, place, sems.at[0, h], sems.at[1, h], copies)
+
+    def scatter(h, copies):
+        def source(owner, lo, hi):
+            return partial.at[h, pl.ds(pl.multiple_of(owner * rows + lo, 16), hi - lo), :]
+
+        def come(offset, lo, hi):
+            return land.at[h, offset, lo:hi, :]
+
+        def leave(offset, lo, hi):
+            return outgoing.at[h, offset, lo:hi, :]
+
+        def done(lo, hi, value):
+            text_out[lo:hi, lanes(h)] = value.astype(text_out.dtype)
+
+        sems = scatter_sems
+        return collect_steps(
+            pieces, source, come, leave, done, sems.at[0, h], sems.at[1, h], copies
+        )
+
+    def work(h, copies):
+        def swap(phase, number, src, dst):
+            copy = pltpu.make_async_remote_copy(
+                src_ref=src,
+                dst_ref=dst,
+                send_sem=pair_sems.at[0, h, phase, number],
+                recv_sem=pair_sems.at[1, h, phase, number],
+                device_id=sibling,
+                device_id_type=MESH,
+            )
+            copy.start()
+            copies[phase, number] = copy
+
+        sent = False
+        for turn in range(column_tiles):
+            c = core * turn + (1 - core) * (column_tiles - 1 - turn)
+            into = pl.ds(pl.multiple_of(c * width, width), width)
+            for r in range(row_tiles):
+                product = lax.dot_general(
+                    tiles[table[r * column_tiles + c]],
+                    panel[h, r * width : (r + 1) * width, :],
+                    (((0,), (0,)), ((), ())),
+                    preferred_element_type=jnp.float32,
+                )
+                if r == 0:
+                    total[into, :] = product
+                else:
+                    total[into, :] += product
+                yield
+            if not sent and (turn + 1) * width >= half:
+                sent = True
+                for number in range(column_tiles):
+                    lo = number * chunk
+                    theirs = pl.ds(pl.multiple_of((1 - core) * half + lo, 16), chunk)
+                    leaving[h, lo : lo + chunk, :] = total[theirs, :].astype(leaving.dtype)
+                    mail = leaving.at[h, lo : lo + chunk, :]
+                    swap(0, number, mail, arrived.at[h, lo : lo + chunk, :])
+        for number in range(column_tiles):
+            lo = number * chunk
+            ours = pl.ds(pl.multiple_of(core * half + lo, 16), chunk)
+            copies[0, number].wait_recv()
+            value = total[ours, :] + arrived[h, lo : lo + chunk, :].astype(jnp.float32)
+            value = value.astype(columns.dtype)
+            columns[h, ours, :] = value
+            tag_out[lo : lo + chunk, lanes(h)] = value
+            swap(1, number, columns.at[h, ours, :], columns.at[h, ours, :])
+            yield
+        for number in range(column_tiles):
+            copies[1, number].wait_recv()
+        for r in range(row_tiles):
+            value = None
+            for c in range(column_tiles):
+                product = jnp.dot(
+                    tiles[table[r * column_tiles + c]],
+                    columns[h, c * width : (c + 1) * width, :],
+                    preferred_element_type=jnp.float32,
+                )
+                value = product if value is None else value + product
+                if c < column_tiles - 1:
+                    yield
+            partial[h, r * width : (r + 1) * width, :] = value.astype(partial.dtype)
+            yield
+
+    gathered, paired, summed = ([{} for _ in range(parts)] for _ in range(3))
+    gathers = [gather(h, gathered[h]) for h in range(parts)]
+    scatters = [scatter(h, summed[h]) for h in range(parts)]
+    advance(gathers[0], 1)
+    tiles[slots] = jnp.zeros((width, width), tiles.dtype)
+    for r in range(row_tiles):
+        for c in range(column_tiles):
+            found = jnp.int32(slots)
+            for slot in range(slots):
+                live = (tile_rows[0, slot] == r) & (tile_cols[0, slot] == c)
+                found = jnp.where(live & (slot < tile_counts[0, 0]), slot, found)
+            table[r * column_tiles + c] = found
+    for h in range(parts):
+        panel[h, pl.ds(pl.multiple_of(me * rows, 16), rows), :] = shard[:, lanes(h)]
+    forwards = len(pieces) * (size // 2 - 1)
+    for h in range(parts):
+        advance(gathers[h], forwards if h == 0 else 0)
+        if h + 1 < parts:
+            advance(gathers[h + 1], 1)
+        finish_steps(gathers[h])
+        if h == 0:
+            load.wait()
+        if h + 1 < parts:
+            weave(work(h, paired[h]), gathers[h + 1], 3, 2)
+        else:
+            weave(work(h, paired[h]), scatters[h - 1] if h else iter(()), 3, 1)
+        advance(scatters[h], 1)
+    for h in range(parts):
+        finish_steps(scatters[h])
+    for copies in gathered + paired + summed:
+        drain(copies)
+
+
+def front(shard, tiles, tile_rows, tile_cols, tile_counts, size):
+    rows, comps = shard.shape
+    slots, width, _ = tiles.shape
+    parts = 2 if comps % (2 * LANES) == 0 else 1
+    part = comps // parts
+    row_span, column_span = rows * size, TC * width
+    half = column_span // 2
+    pieces = hypercube(size, rows, 16)
+    narrow = jnp.bfloat16
+    vmem, smem = pl.BlockSpec(memory_space=VMEM), pl.BlockSpec(memory_space=pltpu.SMEM)
+    return pl.pallas_call(
+        functools.partial(front_kernel, size, pieces),
+        out_shape=(
+            jax.ShapeDtypeStruct((rows, comps), narrow),
+            jax.ShapeDtypeStruct((half, comps), narrow),
+        ),
+        in_specs=[vmem, pl.BlockSpec(memory_space=pltpu.HBM), smem, smem, smem],
+        out_specs=[vmem, vmem],
+        scratch_shapes=[
+            VMEM((slots + 1, width, width), narrow),
+            pltpu.SMEM((row_span // width * TC,), jnp.int32),
+            VMEM((parts, row_span, part), narrow),
+            VMEM((column_span, part), jnp.float32),
+            VMEM((parts, half, part), narrow),
+            VMEM((parts, half, part), narrow),
+            VMEM((parts, column_span, part), narrow),
+            VMEM((parts, row_span, part), narrow),
+            VMEM((parts, size, rows, part), narrow),
+            VMEM((parts, size, rows, part), narrow),
+            pltpu.SemaphoreType.DMA,
+            semaphores(2, parts, len(pieces), size),
+            semaphores(2, parts, 2, TC),
+            semaphores(2, parts, len(pieces), size),
+        ],
+        cost_estimate=pl.CostEstimate(flops=0, bytes_accessed=50_000_000, transcendentals=0),
+        compiler_params=pltpu.CompilerParams(
+            collective_id=5, has_side_effects=True, vmem_limit_bytes=52 << 20
+        ),
+    )(shard, tiles, tile_rows, tile_cols, tile_counts)
 
 
 def lower(blocks):
@@ -623,31 +840,32 @@
     column_span = TC * width
     share = column_span // text_size
     paired = text_size == 2 and LANES // tag_size >= 8
-    row_block = gather(panel_init, tag_size)
-    row_span = row_block.shape[0]
-
-    tag_partial = tile_product(
-        tag_kernel, tiles, rows, cols, count, row_block, column_span, jnp.float32, []
-    )
     if paired:
-        column_block, tag_mine = pair_sum(tag_partial)
+        text_mine, tag_mine = front(
+            panel_init, tiles, tile_rows, tile_cols, tile_counts, tag_size
+        )
     else:
+        row_block = gather(panel_init, tag_size)
+        row_span = row_block.shape[0]
+        tag_partial = tile_product(
+            tag_kernel, tiles, rows, cols, count, row_block, column_span, jnp.float32, []
+        )
         column_block = lax.psum(tag_partial, "text").astype(jnp.bfloat16)
         tag_mine = lax.dynamic_slice_in_dim(
             column_block, lax.axis_index("text") * share, share, 0
         )
-    text_partial = tile_product(
-        text_kernel,
-        tiles,
-        rows,
-        cols,
-        count,
-        column_block,
-        row_span,
-        jnp.bfloat16,
-        [VMEM((row_span, comps), jnp.float32)],
-    )
-    text_mine = scatter_sum(text_partial, tag_size)
+        text_partial = tile_product(
+            text_kernel,
+            tiles,
+            rows,
+            cols,
+            count,
+            column_block,
+            row_span,
+            jnp.bfloat16,
+            [VMEM((row_span, comps), jnp.float32)],
+        )
+        text_mine = scatter_sum(text_partial, tag_size)
     if paired:
         gram = gram_sum(text_mine, tag_mine, tag_size)
         inverses = swap_inverses(inverse_factor(gram))

time: 123 us -> 122 us (level)
    pallas_call x1, Pallas kernels: 31.4 us -> 32.8 us  [gram_sum(): remote_call(functools.partial(gram_kernel, size, pieces), 3, square, [VME...]
    unnamed x10 -> x6, local copies, waits for them, and re-layouts: 3.39 us -> 2.21 us
    pallas_call x5 -> x1, Pallas kernels: 65.8 us -> 65.2 us  [front(): pl.pallas_call(functools.partial(front_kernel, size, pieces), out_shape=(...]
where the time goes in v2:
time: 122 us
  Pallas kernels  118 us (97%)
  local copies, waits for them, and re-layouts  2.21 us (2%)
  between operations  1.32 us (1%)
    pallas_call x1, Pallas kernels, front(): pl.pallas_call(functools.partial(front_kernel, size, pieces), out_shape=(...  65.2 us
    pallas_call x1, Pallas kernels, gram_sum(): remote_call(functools.partial(gram_kernel, size, pieces), 3, square, [VME...  32.8 us
    pallas_call x1, Pallas kernels, inverse_factor(): pl.pallas_call(factor_kernel, out_shape=jax.ShapeDtypeStruct(gram.shape,...  13.9 us
    pallas_call x1, Pallas kernels, whiten(): pl.pallas_call(functools.partial(white_kernel, text_scale, tag_scale), ou...  3.66 us
    pallas_call x1, Pallas kernels, swap_inverses(): remote_call(swap_kernel, 4, jax.ShapeDtypeStruct((2,) + inverse.shape, jn...  2.71 us

profile of v2, /device:TPU:0, one launch (start us, length us, event | category | flops | bytes accessed | tf_op | source)
XLA Modules:
  0.0 121.9 jit_solution(4411075351316011448)
XLA Ops:
  1.3 0.0 copy-start
  1.3 0.9 copy-done
  2.2 0.0 copy-start.1
  2.2 0.7 copy-done.1
  2.8 0.0 copy-start.2
  2.8 0.7 copy-done.2
  3.5 65.2 %shard_map.68 = (bf16[128,512]{1,0:T(8,128)(2,1)S(1)}, bf16[768,512]{1,0:T(8,128)(2,1)S(1)}) custom-call(bf16[128,512]{1,0:T(8,128)(2,1)S(1)} %copy-done, bf16[10,512,512]{2,1,0:T(8,128)(2,1)} %bitcast.1, s32[1,10]{1,0:T(1,128)S(1)} %copy-done.1, s32[1,10]{1,0:T(1,128)S(1)} %copy-done.2, s32[1,1]{1,0:T(1,128)S(6)} %copy.7.tile_counts), custom_call_target="tpu_custom_call" | custom-call | bytes 50000000 | tf_op jit(solution)/shard_map/pallas_call | solution.py:698
  68.7 32.8 %shard_map.69.gram = f32[512,512]{1,0:T(8,128)S(1)} custom-call(bf16[128,512]{1,0:T(8,128)(2,1)S(1)} %get-tuple-element.4.text, bf16[768,512]{1,0:T(8,128)(2,1)S(1)} %get-tuple-element.5.tag), custom_call_target="tpu_custom_call" | custom-call | bytes 50000000 | tf_op jit(solution)/shard_map/pallas_call | solution.py:786
  101.5 13.9 %shard_map.70.inverse = f32[512,512]{1,0:T(8,128)S(1)} custom-call(f32[512,512]{1,0:T(8,128)S(1)} %shard_map.69.gram), custom_call_target="tpu_custom_call" | custom-call | tf_op jit(solution)/shard_map/pallas_call | solution.py:193
  115.5 2.7 %shard_map.71.inverses = f32[2,512,512]{2,1,0:T(8,128)S(1)} custom-call(f32[512,512]{1,0:T(8,128)S(1)} %shard_map.70.inverse), custom_call_target="tpu_custom_call" | custom-call | bytes 50000000 | tf_op jit(solution)/shard_map/pallas_call | solution.py:822
  118.2 3.7 %shard_map.72 = (f32[128,512]{1,0:T(8,128)}, f32[768,512]{1,0:T(8,128)}) custom-call(bf16[128,512]{1,0:T(8,128)(2,1)S(1)} %get-tuple-element.4.text, bf16[768,512]{1,0:T(8,128)(2,1)S(1)} %get-tuple-element.5.tag, f32[2,512,512]{2,1,0:T(8,128)S(1)} %shard_map.71.inverses), custom_call_target="tpu_custom_call" | custom-call | tf_op jit(solution)/shard_map/pallas_call | solution.py:219
Async XLA Ops:
  1.3 0.9 copy-start
  2.2 0.7 copy-start.1
  2.8 0.7 copy-start.2

commit v3 on v2

--- a/solution.py
+++ b/solution.py
@@ -474,10 +474,10 @@
                 copies[number, offset].wait_recv()
                 for later in range(stage + 1, bits):
                     go(number, offset, order[later])
-                yield
-
-
-def collect_steps(pieces, source, land, outgoing, finish, send, recv, copies):
+                yield number, offset
+
+
+def collect_steps(pieces, source, land, outgoing, finish, send, recv, copies, before):
     me = lax.axis_index("tag")
     bits = len(pieces[0][0])
 
@@ -506,7 +506,9 @@
     for turn in reversed(range(1 << last)):
         for number, (order, lo, hi) in enumerate(pieces):
             offset = arrivals(order, last)[turn]
+            before(offset)
             go(number, offset, order[last], source(flip(me, offset), lo, hi))
+    before(0)
     yield
     for stage in reversed(range(last)):
         for turn in reversed(range(1 << stage)):
@@ -521,22 +523,9 @@
         yield
 
 
-def advance(steps, count):
-    for _ in range(count):
-        if next(steps, steps) is steps:
-            return False
-    return True
-
-
 def finish_steps(steps):
     for _ in steps:
         pass
-
-
-def weave(work, steps, lead, ratio):
-    for number, _ in enumerate(work):
-        if number >= lead:
-            advance(steps, ratio)
 
 
 def front_kernel(
@@ -549,113 +538,37 @@
     sibling = {"text": 1 - core}
     slots, width, _ = stored.shape
     rows = shard.shape[0]
-    parts, row_span, part = panel.shape
-    column_span = columns.shape[1]
+    row_span, column_span = panel.shape[0], columns.shape[0]
     row_tiles, column_tiles = row_span // width, column_span // width
+    share = width // rows
     half = column_span // 2
     chunk = half // column_tiles
     load = pltpu.make_async_copy(stored, tiles.at[0:slots], tile_sem)
     load.start()
     greet(tag_partners(size) + [sibling])
 
-    def lanes(h):
-        return slice(h * part, (h + 1) * part)
-
-    def gather(h, copies):
-        def place(owner, lo, hi):
-            return panel.at[h, pl.ds(pl.multiple_of(owner * rows + lo, 16), hi - lo), :]
-
-        def source(lo, hi):
-            return shard.at[lo:hi, lanes(h)]
-
-        sems = gather_sems
-        return spread_steps(pieces, source, place, sems.at[0, h], sems.at[1, h], copies)
-
-    def scatter(h, copies):
-        def source(owner, lo, hi):
-            return partial.at[h, pl.ds(pl.multiple_of(owner * rows + lo, 16), hi - lo), :]
-
-        def come(offset, lo, hi):
-            return land.at[h, offset, lo:hi, :]
-
-        def leave(offset, lo, hi):
-            return outgoing.at[h, offset, lo:hi, :]
-
-        def done(lo, hi, value):
-            text_out[lo:hi, lanes(h)] = value.astype(text_out.dtype)
-
-        sems = scatter_sems
-        return collect_steps(
-            pieces, source, come, leave, done, sems.at[0, h], sems.at[1, h], copies
-        )
-
-    def work(h, copies):
-        def swap(phase, number, src, dst):
-            copy = pltpu.make_async_remote_copy(
-                src_ref=src,
-                dst_ref=dst,
-                send_sem=pair_sems.at[0, h, phase, number],
-                recv_sem=pair_sems.at[1, h, phase, number],
-                device_id=sibling,
-                device_id_type=MESH,
-            )
-            copy.start()
-            copies[phase, number] = copy
-
-        sent = False
-        for turn in range(column_tiles):
-            c = core * turn + (1 - core) * (column_tiles - 1 - turn)
-            into = pl.ds(pl.multiple_of(c * width, width), width)
-            for r in range(row_tiles):
-                product = lax.dot_general(
-                    tiles[table[r * column_tiles + c]],
-                    panel[h, r * width : (r + 1) * width, :],
-                    (((0,), (0,)), ((), ())),
-                    preferred_element_type=jnp.float32,
-                )
-                if r == 0:
-                    total[into, :] = product
-                else:
-                    total[into, :] += product
-                yield
-            if not sent and (turn + 1) * width >= half:
-                sent = True
-                for number in range(column_tiles):
-                    lo = number * chunk
-                    theirs = pl.ds(pl.multiple_of((1 - core) * half + lo, 16), chunk)
-                    leaving[h, lo : lo + chunk, :] = total[theirs, :].astype(leaving.dtype)
-                    mail = leaving.at[h, lo : lo + chunk, :]
-                    swap(0, number, mail, arrived.at[h, lo : lo + chunk, :])
-        for number in range(column_tiles):
-            lo = number * chunk
-            ours = pl.ds(pl.multiple_of(core * half + lo, 16), chunk)
-            copies[0, number].wait_recv()
-            value = total[ours, :] + arrived[h, lo : lo + chunk, :].astype(jnp.float32)
-            value = value.astype(columns.dtype)
-            columns[h, ours, :] = value
-            tag_out[lo : lo + chunk, lanes(h)] = value
-            swap(1, number, columns.at[h, ours, :], columns.at[h, ours, :])
-            yield
-        for number in range(column_tiles):
-            copies[1, number].wait_recv()
-        for r in range(row_tiles):
-            value = None
-            for c in range(column_tiles):
-                product = jnp.dot(
-                    tiles[table[r * column_tiles + c]],
-                    columns[h, c * width : (c + 1) * width, :],
-                    preferred_element_type=jnp.float32,
-                )
-                value = product if value is None else value + product
-                if c < column_tiles - 1:
-                    yield
-            partial[h, r * width : (r + 1) * width, :] = value.astype(partial.dtype)
-            yield
-
-    gathered, paired, summed = ([{} for _ in range(parts)] for _ in range(3))
-    gathers = [gather(h, gathered[h]) for h in range(parts)]
-    scatters = [scatter(h, summed[h]) for h in range(parts)]
-    advance(gathers[0], 1)
+    def place(owner, lo, hi):
+        return panel.at[pl.ds(pl.multiple_of(owner * rows + lo, 16), hi - lo), :]
+
+    def source(owner, lo, hi):
+        return partial.at[pl.ds(pl.multiple_of(owner * rows + lo, 16), hi - lo), :]
+
+    def row_tile(distance):
+        return lax.div(flip(me, distance * share), share)
+
+    def tile_rows_of(r):
+        return pl.ds(pl.multiple_of(r * width, width), width)
+
+    gathered, paired, summed = {}, {}, {}
+    steps = spread_steps(
+        pieces,
+        lambda lo, hi: shard.at[lo:hi, :],
+        place,
+        gather_sems.at[0],
+        gather_sems.at[1],
+        gathered,
+    )
+    next(steps)
     tiles[slots] = jnp.zeros((width, width), tiles.dtype)
     for r in range(row_tiles):
         for c in range(column_tiles):
@@ -664,32 +577,110 @@
                 live = (tile_rows[0, slot] == r) & (tile_cols[0, slot] == c)
                 found = jnp.where(live & (slot < tile_counts[0, 0]), slot, found)
             table[r * column_tiles + c] = found
-    for h in range(parts):
-        panel[h, pl.ds(pl.multiple_of(me * rows, 16), rows), :] = shard[:, lanes(h)]
-    forwards = len(pieces) * (size // 2 - 1)
-    for h in range(parts):
-        advance(gathers[h], forwards if h == 0 else 0)
-        if h + 1 < parts:
-            advance(gathers[h + 1], 1)
-        finish_steps(gathers[h])
-        if h == 0:
+    panel[pl.ds(pl.multiple_of(me * rows, 16), rows), :] = shard[...]
+
+    def swap(phase, number, src, dst):
+        copy = pltpu.make_async_remote_copy(
+            src_ref=src,
+            dst_ref=dst,
+            send_sem=pair_sems.at[0, phase, number],
+            recv_sem=pair_sems.at[1, phase, number],
+            device_id=sibling,
+            device_id_type=MESH,
+        )
+        copy.start()
+        paired[phase, number] = copy
+
+    finished = []
+
+    def tag_products(distance):
+        if not finished:
             load.wait()
-        if h + 1 < parts:
-            weave(work(h, paired[h]), gathers[h + 1], 3, 2)
-        else:
-            weave(work(h, paired[h]), scatters[h - 1] if h else iter(()), 3, 1)
-        advance(scatters[h], 1)
-    for h in range(parts):
-        finish_steps(scatters[h])
-    for copies in gathered + paired + summed:
+        r = row_tile(distance)
+        block = panel[tile_rows_of(r), :]
+        sent = False
+        for turn in range(column_tiles):
+            c = core * turn + (1 - core) * (column_tiles - 1 - turn)
+            product = lax.dot_general(
+                tiles[table[r * column_tiles + c]],
+                block,
+                (((0,), (0,)), ((), ())),
+                preferred_element_type=jnp.float32,
+            )
+            if not finished:
+                total[tile_rows_of(c), :] = product
+            else:
+                total[tile_rows_of(c), :] += product
+            if len(finished) == row_tiles - 1 and not sent and (turn + 1) * width >= half:
+                sent = True
+                for number in range(column_tiles):
+                    lo = number * chunk
+                    theirs = pl.ds(pl.multiple_of((1 - core) * half + lo, 16), chunk)
+                    leaving[lo : lo + chunk, :] = total[theirs, :].astype(leaving.dtype)
+                    swap(0, number, leaving.at[lo : lo + chunk, :], arrived.at[lo : lo + chunk, :])
+        finished.append(distance)
+
+    missing = {(number, offset) for number in range(len(pieces)) for offset in range(1, size)}
+    for event in steps:
+        missing.discard(event)
+        waiting = {offset // share for _, offset in missing}
+        for distance in range(row_tiles):
+            if distance not in waiting and distance not in finished:
+                tag_products(distance)
+
+    for number in range(column_tiles):
+        lo = number * chunk
+        ours = pl.ds(pl.multiple_of(core * half + lo, 16), chunk)
+        paired[0, number].wait_recv()
+        value = total[ours, :] + arrived[lo : lo + chunk, :].astype(jnp.float32)
+        value = value.astype(columns.dtype)
+        columns[ours, :] = value
+        tag_out[lo : lo + chunk, :] = value
+        swap(1, number, columns.at[ours, :], columns.at[ours, :])
+    for number in range(column_tiles):
+        paired[1, number].wait_recv()
+
+    ready = set()
+
+    def text_products(offset):
+        for distance in [offset // share] if offset else range(row_tiles):
+            if distance in ready:
+                continue
+            ready.add(distance)
+            r = row_tile(distance)
+            value = None
+            for c in range(column_tiles):
+                product = jnp.dot(
+                    tiles[table[r * column_tiles + c]],
+                    columns[c * width : (c + 1) * width, :],
+                    preferred_element_type=jnp.float32,
+                )
+                value = product if value is None else value + product
+            partial[tile_rows_of(r), :] = value.astype(partial.dtype)
+
+    def done(lo, hi, value):
+        text_out[lo:hi, :] = value.astype(text_out.dtype)
+
+    finish_steps(
+        collect_steps(
+            pieces,
+            source,
+            lambda offset, lo, hi: land.at[offset, lo:hi, :],
+            lambda offset, lo, hi: outgoing.at[offset, lo:hi, :],
+            done,
+            scatter_sems.at[0],
+            scatter_sems.at[1],
+            summed,
+            text_products,
+        )
+    )
+    for copies in (gathered, paired, summed):
         drain(copies)
 
 
 def front(shard, tiles, tile_rows, tile_cols, tile_counts, size):
     rows, comps = shard.shape
     slots, width, _ = tiles.shape
-    parts = 2 if comps % (2 * LANES) == 0 else 1
-    part = comps // parts
     row_span, column_span = rows * size, TC * width
     half = column_span // 2
     pieces = hypercube(size, rows, 16)
@@ -706,18 +697,18 @@
         scratch_shapes=[
             VMEM((slots + 1, width, width), narrow),
             pltpu.SMEM((row_span // width * TC,), jnp.int32),
-            VMEM((parts, row_span, part), narrow),
-            VMEM((column_span, part), jnp.float32),
-            VMEM((parts, half, part), narrow),
-            VMEM((parts, half, part), narrow),
-            VMEM((parts, column_span, part), narrow),
-            VMEM((parts, row_span, part), narrow),
-            VMEM((parts, size, rows, part), narrow),
-            VMEM((parts, size, rows, part), narrow),
+            VMEM((row_span, comps), narrow),
+            VMEM((column_span, comps), jnp.float32),
+            VMEM((half, comps), narrow),
+            VMEM((half, comps), narrow),
+            VMEM((column_span, comps), narrow),
+            VMEM((row_span, comps), narrow),
+            VMEM((size, rows, comps), narrow),
+            VMEM((size, rows, comps), narrow),
             pltpu.SemaphoreType.DMA,
-            semaphores(2, parts, len(pieces), size),
-            semaphores(2, parts, 2, TC),
-            semaphores(2, parts, len(pieces), size),
+            semaphores(2, len(pieces), size),
+            semaphores(2, 2, TC),
+            semaphores(2, len(pieces), size),
         ],
         cost_estimate=pl.CostEstimate(flops=0, bytes_accessed=50_000_000, transcendentals=0),
         compiler_params=pltpu.CompilerParams(
@@ -762,8 +753,20 @@
     def finish(lo, hi, total):
         own[lo:hi] = total
 
-    copies = collect_start(pieces, source, land, sems.at[0], sems.at[1])
-    collect(pieces, copies, source, land, outgoing, finish, sems.at[0], sems.at[1])
+    copies = {}
+    finish_steps(
+        collect_steps(
+            pieces,
+            source,
+            lambda offset, lo, hi: land.at[offset, lo:hi],
+            lambda offset, lo, hi: outgoing.at[offset, lo:hi],
+            finish,
+            sems.at[0],
+            sems.at[1],
+            copies,
+            lambda offset: None,
+        )
+    )
     more = spread(pieces, lambda lo, hi: own.at[lo:hi], place, sems.at[2], sems.at[3])
     gathered[:, pl.ds(pl.multiple_of(me * rows, 8), rows), :] = own[...]
     drain(copies)

time: 122 us -> 107 us (0.88)
  Pallas kernels: 118 us -> 104 us
    pallas_call x1, Pallas kernels: 65.2 us -> 53.1 us  [front(): pl.pallas_call(functools.partial(front_kernel, size, pieces), out_shape=(...]
    pallas_call x1, Pallas kernels: 32.8 us -> 30.1 us  [gram_sum(): remote_call(functools.partial(gram_kernel, size, pieces), 3, square, [VME...]
where the time goes in v3:
time: 107 us
  Pallas kernels  104 us (97%)
  local copies, waits for them, and re-layouts  2.21 us (2%)
  between operations  1.32 us (1%)
    pallas_call x1, Pallas kernels, front(): pl.pallas_call(functools.partial(front_kernel, size, pieces), out_shape=(...  53.1 us
    pallas_call x1, Pallas kernels, gram_sum(): remote_call(functools.partial(gram_kernel, size, pieces), 3, square, [VME...  30.1 us
    pallas_call x1, Pallas kernels, inverse_factor(): pl.pallas_call(factor_kernel, out_shape=jax.ShapeDtypeStruct(gram.shape,...  13.9 us
    pallas_call x1, Pallas kernels, whiten(): pl.pallas_call(functools.partial(white_kernel, text_scale, tag_scale), ou...  3.65 us
    pallas_call x1, Pallas kernels, swap_inverses(): remote_call(swap_kernel, 4, jax.ShapeDtypeStruct((2,) + inverse.shape, jn...  2.71 us
    unnamed x6, local copies, waits for them, and re-layouts  2.21 us

profile of v3, /device:TPU:0, one launch (start us, length us, event | category | flops | bytes accessed | tf_op | source)
XLA Modules:
  0.0 107.0 jit_solution(3856212852902754430)
XLA Ops:
  1.3 0.0 copy-start
  1.3 0.9 copy-done
  2.2 0.0 copy-start.1
  2.2 0.7 copy-done.1
  2.8 0.0 copy-start.2
  2.8 0.7 copy-done.2
  3.5 53.1 %shard_map.68 = (bf16[128,512]{1,0:T(8,128)(2,1)S(1)}, bf16[768,512]{1,0:T(8,128)(2,1)S(1)}) custom-call(bf16[128,512]{1,0:T(8,128)(2,1)S(1)} %copy-done, bf16[10,512,512]{2,1,0:T(8,128)(2,1)} %bitcast.1, s32[1,10]{1,0:T(1,128)S(1)} %copy-done.1, s32[1,10]{1,0:T(1,128)S(1)} %copy-done.2, s32[1,1]{1,0:T(1,128)S(6)} %copy.7.tile_counts), custom_call_target="tpu_custom_call" | custom-call | bytes 50000000 | tf_op jit(solution)/shard_map/pallas_call | solution.py:689
  56.6 30.1 %shard_map.69.gram = f32[512,512]{1,0:T(8,128)S(1)} custom-call(bf16[128,512]{1,0:T(8,128)(2,1)S(1)} %get-tuple-element.4.text, bf16[768,512]{1,0:T(8,128)(2,1)S(1)} %get-tuple-element.5.tag), custom_call_target="tpu_custom_call" | custom-call | bytes 50000000 | tf_op jit(solution)/shard_map/pallas_call | solution.py:789
  86.8 13.9 %shard_map.70.inverse = f32[512,512]{1,0:T(8,128)S(1)} custom-call(f32[512,512]{1,0:T(8,128)S(1)} %shard_map.69.gram), custom_call_target="tpu_custom_call" | custom-call | tf_op jit(solution)/shard_map/pallas_call | solution.py:193
  100.7 2.7 %shard_map.71.inverses = f32[2,512,512]{2,1,0:T(8,128)S(1)} custom-call(f32[512,512]{1,0:T(8,128)S(1)} %shard_map.70.inverse), custom_call_target="tpu_custom_call" | custom-call | bytes 50000000 | tf_op jit(solution)/shard_map/pallas_call | solution.py:825
  103.4 3.7 %shard_map.72 = (f32[128,512]{1,0:T(8,128)}, f32[768,512]{1,0:T(8,128)}) custom-call(bf16[128,512]{1,0:T(8,128)(2,1)S(1)} %get-tuple-element.4.text, bf16[768,512]{1,0:T(8,128)(2,1)S(1)} %get-tuple-element.5.tag, f32[2,512,512]{2,1,0:T(8,128)S(1)} %shard_map.71.inverses), custom_call_target="tpu_custom_call" | custom-call | tf_op jit(solution)/shard_map/pallas_call | solution.py:219
Async XLA Ops:
  1.3 0.9 copy-start
  2.2 0.7 copy-start.1
  2.8 0.7 copy-start.2

commit v4 on v3

--- a/solution.py
+++ b/solution.py
@@ -146,7 +146,7 @@
     return jnp.concatenate(out, axis=0)
 
 
-def factor_in_place(work, scale, out):
+def factor_in_place(work, scale, store):
     size = work.shape[0]
     blocks = size // LANES
     exact = lax.Precision.HIGHEST
@@ -181,12 +181,15 @@
             )
         lanes = lax.broadcasted_iota(jnp.int32, (LANES, size), 1)
         subs = lax.broadcasted_iota(jnp.int32, (LANES, size), 0) + lo
-        out[lo:hi, :] = jnp.where(lanes <= subs, work[lo:hi, :] * scale[...], 0.0)
+        store(lo, hi, jnp.where(lanes <= subs, work[lo:hi, :] * scale[...], 0.0))
 
 
 def factor_kernel(gram, out, work, scale):
+    def store(lo, hi, value):
+        out[lo:hi, :] = value
+
     work[...] = gram[...]
-    factor_in_place(work, scale, out)
+    factor_in_place(work, scale, store)
 
 
 def inverse_factor(gram):
@@ -523,15 +526,20 @@
         yield
 
 
+def advance(steps, count):
+    for _ in range(count):
+        next(steps, None)
+
+
 def finish_steps(steps):
     for _ in steps:
         pass
 
 
 def front_kernel(
-    size, pieces, shard, stored, tile_rows, tile_cols, tile_counts, text_out, tag_out,
+    size, pieces, shard, stored, tile_rows, tile_cols, tile_counts, text_out, tag_out, tag_gram,
     tiles, table, panel, total, leaving, arrived, columns, partial, land, outgoing,
-    tile_sem, gather_sems, pair_sems, scatter_sems,
+    tile_sem, gather_sems, pair_sems, scatter_sems, *gram_refs,
 ):
     core = lax.axis_index("text")
     me = lax.axis_index("tag")
@@ -640,6 +648,13 @@
     for number in range(column_tiles):
         paired[1, number].wait_recv()
 
+    grams = [{}, {}]
+    both, mine, own, gram_land, gram_outgoing, gram_pair, gram_sems = gram_refs
+    tag_steps = gram_steps(
+        size, tag_out, both, mine, own, tag_gram, gram_land, gram_outgoing,
+        gram_pair, gram_sems, grams,
+    )
+    next(tag_steps)
     ready = set()
 
     def text_products(offset):
@@ -657,24 +672,26 @@
                 )
                 value = product if value is None else value + product
             partial[tile_rows_of(r), :] = value.astype(partial.dtype)
+            advance(tag_steps, 6)
 
     def done(lo, hi, value):
         text_out[lo:hi, :] = value.astype(text_out.dtype)
 
-    finish_steps(
-        collect_steps(
-            pieces,
-            source,
-            lambda offset, lo, hi: land.at[offset, lo:hi, :],
-            lambda offset, lo, hi: outgoing.at[offset, lo:hi, :],
-            done,
-            scatter_sems.at[0],
-            scatter_sems.at[1],
-            summed,
-            text_products,
-        )
-    )
-    for copies in (gathered, paired, summed):
+    scatter_steps = collect_steps(
+        pieces,
+        source,
+        lambda offset, lo, hi: land.at[offset, lo:hi, :],
+        lambda offset, lo, hi: outgoing.at[offset, lo:hi, :],
+        done,
+        scatter_sems.at[0],
+        scatter_sems.at[1],
+        summed,
+        text_products,
+    )
+    for _ in scatter_steps:
+        advance(tag_steps, 2)
+    finish_steps(tag_steps)
+    for copies in (gathered, paired, summed, *grams):
         drain(copies)
 
 
@@ -683,6 +700,7 @@
     slots, width, _ = tiles.shape
     row_span, column_span = rows * size, TC * width
     half = column_span // 2
+    blocks = len(lower(comps // LANES))
     pieces = hypercube(size, rows, 16)
     narrow = jnp.bfloat16
     vmem, smem = pl.BlockSpec(memory_space=VMEM), pl.BlockSpec(memory_space=pltpu.SMEM)
@@ -691,9 +709,10 @@
         out_shape=(
             jax.ShapeDtypeStruct((rows, comps), narrow),
             jax.ShapeDtypeStruct((half, comps), narrow),
+            jax.ShapeDtypeStruct((blocks // 2, LANES, LANES), jnp.float32),
         ),
         in_specs=[vmem, pl.BlockSpec(memory_space=pltpu.HBM), smem, smem, smem],
-        out_specs=[vmem, vmem],
+        out_specs=[vmem, vmem, vmem],
         scratch_shapes=[
             VMEM((slots + 1, width, width), narrow),
             pltpu.SMEM((row_span // width * TC,), jnp.int32),
@@ -709,6 +728,7 @@
             semaphores(2, len(pieces), size),
             semaphores(2, 2, TC),
             semaphores(2, len(pieces), size),
+            *gram_scratch(comps, size),
         ],
         cost_estimate=pl.CostEstimate(flops=0, bytes_accessed=50_000_000, transcendentals=0),
         compiler_params=pltpu.CompilerParams(
@@ -721,114 +741,157 @@
     return [(i, j) for i in range(blocks) for j in range(i + 1)]
 
 
-def gram_kernel(size, pieces, text, tag, out, both, other, own, gathered, land, outgoing, pair, sems):
+def gram_steps(size, panel, both, mine, own, gathered, land, outgoing, pair, sems, copies):
     core = lax.axis_index("text")
     me = lax.axis_index("tag")
     rows = own.shape[1]
-    pairs = lower(out.shape[0] // LANES)
-    sibling = {"text": 1 - core}
-    greet(tag_partners(size) + [sibling])
-    for kind, panel in ((0, text), (1, tag)):
-        gram = local_gram(panel[...])
-        for at, (i, j) in enumerate(pairs):
-            both[kind, at] = gram[i * LANES : (i + 1) * LANES, j * LANES : (j + 1) * LANES]
+    share = mine.shape[0]
+    pieces = hypercube(size, share, 1)
+    gram = local_gram(panel[...])
+    for at, (i, j) in enumerate(lower(gram.shape[0] // LANES)):
+        both[at] = gram[i * LANES : (i + 1) * LANES, j * LANES : (j + 1) * LANES]
     swap = pltpu.make_async_remote_copy(
-        src_ref=both.at[1 - core],
-        dst_ref=other,
+        src_ref=both.at[pl.ds((1 - core) * share, share)],
+        dst_ref=mine,
         send_sem=pair.at[0],
         recv_sem=pair.at[1],
+        device_id={"text": 1 - core},
+        device_id_type=MESH,
+    )
+    swap.start()
+    yield
+    swap.wait()
+    mine[...] += both[pl.ds(core * share, share)]
+
+    def place(owner, lo, hi):
+        return gathered.at[lo:hi, pl.ds(pl.multiple_of(owner * rows, 8), rows), :]
+
+    def source(owner, lo, hi):
+        return mine.at[lo:hi, pl.ds(pl.multiple_of(owner * rows, 8), rows), :]
+
+    def finish(lo, hi, total):
+        own[lo:hi] = total
+
+    yield from collect_steps(
+        pieces,
+        source,
+        lambda offset, lo, hi: land.at[offset, lo:hi],
+        lambda offset, lo, hi: outgoing.at[offset, lo:hi],
+        finish,
+        sems.at[0],
+        sems.at[1],
+        copies[0],
+        lambda offset: None,
+    )
+    yield from spread_steps(
+        pieces, lambda lo, hi: own.at[lo:hi], place, sems.at[2], sems.at[3], copies[1]
+    )
+    gathered[:, pl.ds(pl.multiple_of(me * rows, 8), rows), :] = own[...]
+
+
+def gram_scratch(comps, size):
+    count = len(lower(comps // LANES))
+    share, rows = count // 2, LANES // size
+    pieces = hypercube(size, share, 1)
+    return [
+        VMEM((count, LANES, LANES), jnp.float32),
+        VMEM((share, LANES, LANES), jnp.float32),
+        VMEM((share, rows, LANES), jnp.float32),
+        VMEM((size, share, rows, LANES), jnp.float32),
+        VMEM((size, share, rows, LANES), jnp.float32),
+        semaphores(2),
+        semaphores(4, len(pieces), size),
+    ]
+
+
+def gram_kernel(
+    size, text, tag, out, halves, whole, both, mine, own, land, outgoing, pair, sems, last
+):
+    core = lax.axis_index("text")
+    sibling = {"text": 1 - core}
+    share = tag.shape[0]
+    greet(tag_partners(size) + [sibling])
+    copies = [{}, {}]
+    finish_steps(
+        gram_steps(
+            size, text, both, mine, own, halves.at[0], land, outgoing, pair, sems, copies
+        )
+    )
+    halves[1] = tag[...]
+    swap = pltpu.make_async_remote_copy(
+        src_ref=halves.at[1 - core],
+        dst_ref=whole.at[pl.ds(core * share, share)],
+        send_sem=last.at[0],
+        recv_sem=last.at[1],
         device_id=sibling,
         device_id_type=MESH,
     )
     swap.start()
+    whole[pl.ds(core * share, share)] = halves[core]
     swap.wait()
-    other[...] += both[core]
-
-    def place(owner, lo, hi):
-        return gathered.at[lo:hi, pl.ds(pl.multiple_of(owner * rows, 8), rows), :]
-
-    def source(owner, lo, hi):
-        return other.at[lo:hi, pl.ds(pl.multiple_of(owner * rows, 8), rows), :]
-
-    def finish(lo, hi, total):
-        own[lo:hi] = total
-
-    copies = {}
-    finish_steps(
-        collect_steps(
-            pieces,
-            source,
-            lambda offset, lo, hi: land.at[offset, lo:hi],
-            lambda offset, lo, hi: outgoing.at[offset, lo:hi],
-            finish,
-            sems.at[0],
-            sems.at[1],
-            copies,
-            lambda offset: None,
-        )
-    )
-    more = spread(pieces, lambda lo, hi: own.at[lo:hi], place, sems.at[2], sems.at[3])
-    gathered[:, pl.ds(pl.multiple_of(me * rows, 8), rows), :] = own[...]
-    drain(copies)
-    drain(more)
-    for at, (i, j) in enumerate(pairs):
-        block = gathered[at]
-        if i == j:
-            out[i * LANES : (i + 1) * LANES, j * LANES : (j + 1) * LANES] = block
-        else:
+    for group in copies:
+        drain(group)
+    for at, (i, j) in enumerate(lower(out.shape[0] // LANES)):
+        block = whole[at]
+        if i != j:
             out[j * LANES : (j + 1) * LANES, i * LANES : (i + 1) * LANES] = block.T
-            out[i * LANES : (i + 1) * LANES, j * LANES : (j + 1) * LANES] = block
+        out[i * LANES : (i + 1) * LANES, j * LANES : (j + 1) * LANES] = block
 
 
 def gram_sum(text, tag, size):
     comps = text.shape[1]
-    rows = LANES // size
-    count = len(lower(comps // LANES))
-    pieces = hypercube(size, count, 1)
-    square = jax.ShapeDtypeStruct((comps, comps), jnp.float32)
+    share = tag.shape[0]
     return remote_call(
-        functools.partial(gram_kernel, size, pieces),
+        functools.partial(gram_kernel, size),
         3,
-        square,
+        jax.ShapeDtypeStruct((comps, comps), jnp.float32),
         [
-            VMEM((2, count, LANES, LANES), jnp.float32),
-            VMEM((count, LANES, LANES), jnp.float32),
-            VMEM((count, rows, LANES), jnp.float32),
-            VMEM((count, LANES, LANES), jnp.float32),
-            VMEM((size, count, rows, LANES), jnp.float32),
-            VMEM((size, count, rows, LANES), jnp.float32),
+            VMEM((2, share, LANES, LANES), jnp.float32),
+            VMEM((2 * share, LANES, LANES), jnp.float32),
+            *gram_scratch(comps, size),
             semaphores(2),
-            semaphores(4, len(pieces), size),
         ],
         2,
     )(text, tag)
 
 
-def swap_kernel(inverse, out, sems):
+def factor_swap_kernel(gram, out, work, scale, sems):
     core = lax.axis_index("text")
     sibling = {"text": 1 - core}
     greet([sibling])
-    swap = pltpu.make_async_remote_copy(
-        src_ref=inverse,
-        dst_ref=out.at[core],
-        send_sem=sems.at[0],
-        recv_sem=sems.at[1],
-        device_id=sibling,
-        device_id_type=MESH,
-    )
-    swap.start()
-    out[core] = inverse[...]
-    swap.wait()
-
-
-def swap_inverses(inverse):
+    copies = []
+
+    def store(lo, hi, value):
+        out[core, lo:hi, :] = value
+        copy = pltpu.make_async_remote_copy(
+            src_ref=out.at[core, lo:hi, :],
+            dst_ref=out.at[core, lo:hi, :],
+            send_sem=sems.at[0, len(copies)],
+            recv_sem=sems.at[1, len(copies)],
+            device_id=sibling,
+            device_id_type=MESH,
+        )
+        copy.start()
+        copies.append(copy)
+
+    work[...] = gram[...]
+    factor_in_place(work, scale, store)
+    for copy in copies:
+        copy.wait()
+
+
+def inverse_factors(gram):
     return remote_call(
-        swap_kernel,
+        factor_swap_kernel,
         4,
-        jax.ShapeDtypeStruct((2,) + inverse.shape, jnp.float32),
-        [semaphores(2)],
+        jax.ShapeDtypeStruct((2,) + gram.shape, jnp.float32),
+        [
+            VMEM(gram.shape, jnp.float32),
+            VMEM((1, gram.shape[1]), jnp.float32),
+            semaphores(2, gram.shape[0] // LANES),
+        ],
         1,
-    )(inverse)
+    )(gram)
 
 
 def shards(tile_values, tile_rows, tile_cols, tile_counts, panel_init):
@@ -842,9 +905,10 @@
     tag_size = lax.axis_size("tag")
     column_span = TC * width
     share = column_span // text_size
-    paired = text_size == 2 and LANES // tag_size >= 8
+    blocks = len(lower(comps // LANES))
+    paired = text_size == 2 and LANES // tag_size >= 8 and blocks % 2 == 0
     if paired:
-        text_mine, tag_mine = front(
+        text_mine, tag_mine, tag_gram = front(
             panel_init, tiles, tile_rows, tile_cols, tile_counts, tag_size
         )
     else:
@@ -870,8 +934,7 @@
         )
         text_mine = scatter_sum(text_partial, tag_size)
     if paired:
-        gram = gram_sum(text_mine, tag_mine, tag_size)
-        inverses = swap_inverses(inverse_factor(gram))
+        inverses = inverse_factors(gram_sum(text_mine, tag_gram, tag_size))
     else:
         text_gram, tag_gram = lax.psum(
             (local_gram(text_mine), local_gram(tag_mine)), ("text", "tag")

time: 107 us -> 121 us (1.13)
  Pallas kernels: 104 us -> 117 us
    pallas_call x1, Pallas kernels: 53.1 us -> 66.2 us  [front(): pl.pallas_call(functools.partial(front_kernel, size, pieces), out_shape=(...]
    pallas_call x3 -> x2, Pallas kernels: 46.8 us -> 47.2 us  [the longest x1 31.7 us: gram_sum(): remote_call(functools.partial(gram_kernel, size), 3, jax.ShapeDtypeStruct...]
where the time goes in v4:
time: 121 us
  Pallas kernels  117 us (97%)
  local copies, waits for them, and re-layouts  2.21 us (2%)
  between operations  1.31 us (1%)
    pallas_call x1, Pallas kernels, front(): pl.pallas_call(functools.partial(front_kernel, size, pieces), out_shape=(...  66.2 us
    pallas_call x1, Pallas kernels, gram_sum(): remote_call(functools.partial(gram_kernel, size), 3, jax.ShapeDtypeStruct...  31.7 us
    pallas_call x1, Pallas kernels, inverse_factors(): remote_call(factor_swap_kernel, 4, jax.ShapeDtypeStruct((2,) + gram.shape...  15.5 us
    pallas_call x1, Pallas kernels, whiten(): pl.pallas_call(functools.partial(white_kernel, text_scale, tag_scale), ou...  3.65 us

profile of v4, /device:TPU:0, one launch (start us, length us, event | category | flops | bytes accessed | tf_op | source)
XLA Modules:
  0.0 120.6 jit_solution(14482568735429032744)
XLA Ops:
  1.3 0.0 copy-start
  1.3 0.9 copy-done
  2.2 0.0 copy-start.1
  2.2 0.7 copy-done.1
  2.8 0.0 copy-start.2
  2.8 0.7 copy-done.2
  3.5 66.2 %shard_map.68 = (bf16[128,512]{1,0:T(8,128)(2,1)S(1)}, bf16[768,512]{1,0:T(8,128)(2,1)S(1)}, f32[5,128,128]{2,1,0:T(8,128)S(1)}) custom-call(bf16[128,512]{1,0:T(8,128)(2,1)S(1)} %copy-done, bf16[10,512,512]{2,1,0:T(8,128)(2,1)} %bitcast.1, s32[1,10]{1,0:T(1,128)S(1)} %copy-done.1, s32[1,10]{1,0:T(1,128)S(1)} %copy-done.2, s32[1,1]{1,0:T(1,128)S(6)} %copy.7.tile_counts), custom_call_target="tpu_custom_call" | custom-call | bytes 50000000 | tf_op jit(solution)/shard_map/pallas_call | solution.py:707
  69.7 31.7 %shard_map.69.gram = f32[512,512]{1,0:T(8,128)S(1)} custom-call(bf16[128,512]{1,0:T(8,128)(2,1)S(1)} %get-tuple-element.5.text, f32[5,128,128]{2,1,0:T(8,128)S(1)} %get-tuple-element.7.tag), custom_call_target="tpu_custom_call" | custom-call | bytes 50000000 | tf_op jit(solution)/shard_map/pallas_call | solution.py:844
  101.4 15.5 %shard_map.70.inverses = f32[2,512,512]{2,1,0:T(8,128)S(1)} custom-call(f32[512,512]{1,0:T(8,128)S(1)} %shard_map.69.gram), custom_call_target="tpu_custom_call" | custom-call | bytes 50000000 | tf_op jit(solution)/shard_map/pallas_call | solution.py:884
  116.9 3.7 %shard_map.71 = (f32[128,512]{1,0:T(8,128)}, f32[768,512]{1,0:T(8,128)}) custom-call(bf16[128,512]{1,0:T(8,128)(2,1)S(1)} %get-tuple-element.5.text, bf16[768,512]{1,0:T(8,128)(2,1)S(1)} %get-tuple-element.6.tag, f32[2,512,512]{2,1,0:T(8,128)S(1)} %shard_map.70.inverses), custom_call_target="tpu_custom_call" | custom-call | tf_op jit(solution)/shard_map/pallas_call | solution.py:222
Async XLA Ops:
  1.3 0.9 copy-start
  2.2 0.7 copy-start.1
  2.8 0.7 copy-start.2
